TPU v7x, 256 devices: a whole 4x4x8 slice. The times are simulated.
256 devices in a mesh: row: 16 (over y, z_lo, core), col: 16 (over x, z_hi).
Axes of the slice: x: 4, y: 4, z: 8 (z_hi: 4, z_lo: 2; z = z_hi * 2 + z_lo), core: 2. Of those that a mesh axis runs over, the one named last changes fastest.
Arguments:
- support_views: float32 [256, 4, 3, 1024], P(('row', 'col')), may hold values from -6 to 6
- support_pick: int32 [256], P(('row', 'col')), may hold values from 0 to 3
- target_views: float32 [256, 4, 3, 1024], P(('row', 'col')), may hold values from -6 to 6
- target_pick: int32 [256], P(('row', 'col')), may hold values from 0 to 3
- support_labels: float32 [256, 10], P(('row', 'col')), may hold values from -6 to 6
- target_labels: int32 [256], replicated, may hold values from 0 to 9
Outputs:
- support_grad: float32 [256, 3, 1024], P(('row', 'col'))
- label_grad: float32 [256, 10], P(('row', 'col'))
- loss: float32 [], replicated
All inputs are finite; a program needn't handle non-finite values.
Results may differ from a plain program's by a relative error of at most 0.00055.
Values sent between devices are 32-bit elements; how exact they have to be, the bound alone decides.
A program may use at most 64 MiB of HBM per device.

v0:
```python
import math

import jax
import jax.numpy as jnp
from jax import lax
from jax.sharding import PartitionSpec as P

SIDE = 32
LAYERS = 3
SUPPORT = 256


bias_variance = 0.1
ridge_scale = 0.1
highest = lax.Precision.HIGHEST


def shifted(surface, offset):
    extent = surface.shape[-1]
    padding = jnp.zeros(surface.shape[:-1] + (abs(offset),), surface.dtype)
    if offset > 0:
        return jnp.concatenate([surface[..., offset:], padding], axis=-1)
    return jnp.concatenate([padding, surface[..., : extent + offset]], axis=-1)


def average(surface):
    column = jnp.arange(surface.shape[-1], dtype=jnp.int32) % SIDE
    rightward = jnp.where(column < SIDE - 1, shifted(surface, 1), 0.0)
    leftward = jnp.where(column > 0, shifted(surface, -1), 0.0)
    across = surface + leftward + rightward
    return (across + shifted(across, SIDE) + shifted(across, -SIDE)) / 9.0


def choose_view(views, picked):
    options = jnp.arange(views.shape[1], dtype=jnp.int32)
    selector = (picked[:, None] == options[None, :]).astype(jnp.float32)
    return jnp.sum(selector[:, :, None, None] * views, axis=1)


def self_maps(images):
    energy = jnp.sum(images * images, axis=1) / images.shape[1]
    current = average(energy) + bias_variance
    stacked = [current]
    for layer in range(1, LAYERS):
        current = average(current) + bias_variance
        stacked.append(current)
    return jnp.stack(stacked, axis=1)


def self_back(images, grad_maps):
    carry = grad_maps[:, -1]
    for layer in range(grad_maps.shape[1] - 2, -1, -1):
        carry = grad_maps[:, layer] + average(carry)
    return average(carry)[:, None, :] * images * (2.0 / images.shape[1])


def arc(kernel_map, first_diag, second_diag):
    scale_map = jnp.sqrt(first_diag * second_diag)
    cosine = jnp.clip(kernel_map / scale_map, -1.0, 1.0)
    sine = jnp.sqrt(1.0 - cosine * cosine)
    angle = jnp.arccos(cosine)
    value = scale_map * (sine + (jnp.pi - angle) * cosine) / jnp.pi
    slope = (jnp.pi - angle) / jnp.pi
    spread = scale_map * sine / (2.0 * jnp.pi)
    return (value, slope, spread)


def pair_forward(first, first_maps, second, second_maps):
    product = first[:, None, 0] * second[None, :, 0]
    for channel in range(1, first.shape[1]):
        product = product + first[:, None, channel] * second[None, :, channel]
    current = average(product / first.shape[1]) + bias_variance
    slopes = []
    spreads = []
    depth = first_maps.shape[1]
    for layer in range(depth):
        value, slope, spread = arc(current, first_maps[:, None, layer], second_maps[None, :, layer])
        slopes.append(slope)
        spreads.append(spread)
        if layer + 1 < depth:
            current = average(value) + bias_variance
    return (jnp.mean(value, axis=-1), slopes, spreads)


def pair_backward(first, first_maps, second, second_maps, weights, want_second):
    kernel, slopes, spreads = pair_forward(first, first_maps, second, second_maps)
    depth = first_maps.shape[1]
    grad = jnp.broadcast_to(weights[:, :, None] / first.shape[-1], slopes[0].shape)
    first_parts = []
    second_parts = []
    for layer in range(depth - 1, -1, -1):
        scaled = grad * spreads[layer]
        first_parts.insert(0, jnp.sum(scaled, axis=1) / first_maps[:, layer])
        if want_second:
            second_parts.insert(0, jnp.sum(scaled, axis=0) / second_maps[:, layer])
        grad = average(grad * slopes[layer])
    first_image = (
        jnp.stack(
            [jnp.sum(grad * second[None, :, channel], axis=1) for channel in range(first.shape[1])],
            axis=1,
        )
        / first.shape[1]
    )
    if not want_second:
        return (first_image, jnp.stack(first_parts, axis=1), None, None)
    second_image = (
        jnp.stack(
            [jnp.sum(grad * first[:, None, channel], axis=0) for channel in range(first.shape[1])],
            axis=1,
        )
        / first.shape[1]
    )
    return (
        first_image,
        jnp.stack(first_parts, axis=1),
        second_image,
        jnp.stack(second_parts, axis=1),
    )


def blocked_kernel(first, first_maps, second, second_maps):
    block_width = math.gcd(second.shape[0], 4)
    block_count = second.shape[0] // block_width

    def one_block(inputs):
        part_images, part_maps = inputs
        kernel, _, _ = pair_forward(first, first_maps, part_images, part_maps)
        return kernel

    pieces = lax.map(
        one_block,
        (
            second.reshape((block_count, block_width) + second.shape[1:]),
            second_maps.reshape((block_count, block_width) + second_maps.shape[1:]),
        ),
    )
    return jnp.transpose(pieces, (1, 0, 2)).reshape(first.shape[0], second.shape[0])


def blocked_backward(first, first_maps, second, second_maps, weights, want_second):
    block_width = math.gcd(second.shape[0], 4)
    block_count = second.shape[0] // block_width
    block_weights = jnp.transpose(
        weights.reshape(first.shape[0], block_count, block_width), (1, 0, 2)
    )

    def one_block(carry, inputs):
        part_images, part_maps, part_weights = inputs
        grad_first, maps_first, grad_second, maps_second = pair_backward(
            first, first_maps, part_images, part_maps, part_weights, want_second
        )
        return ((carry[0] + grad_first, carry[1] + maps_first), (grad_second, maps_second))

    start = (jnp.zeros(first.shape, jnp.float32), jnp.zeros(first_maps.shape, jnp.float32))
    (first_grad, first_map_grad), (second_grad, second_map_grad) = lax.scan(
        one_block,
        start,
        (
            second.reshape((block_count, block_width) + second.shape[1:]),
            second_maps.reshape((block_count, block_width) + second_maps.shape[1:]),
            block_weights,
        ),
    )
    if not want_second:
        return (first_grad, first_map_grad, None, None)
    return (
        first_grad,
        first_map_grad,
        second_grad.reshape(second.shape),
        second_map_grad.reshape(second_maps.shape),
    )


def solve_with(factor, rhs):
    halfway = lax.linalg.triangular_solve(factor, rhs, left_side=True, lower=True)
    return lax.linalg.triangular_solve(
        factor, halfway, left_side=True, lower=True, transpose_a=True
    )


def assemble(tiles, row_count, col_count, own_rows, own_cols):
    shaped = tiles.reshape(row_count, col_count, col_count, own_rows, row_count, own_cols)
    ordered = jnp.transpose(shaped, (0, 2, 3, 4, 1, 5))
    return ordered.reshape(row_count * col_count * own_rows, row_count * col_count * own_cols)


def column_of(matrix, col_index, row_count, col_count, per_device):
    shaped = matrix.reshape(row_count, col_count, per_device, matrix.shape[-1])
    picked = lax.dynamic_index_in_dim(shaped, col_index, 1, keepdims=False)
    return picked.reshape(row_count * per_device, matrix.shape[-1])


def body(support_views, support_pick, target_views, target_pick, support_labels, target_labels):
    row_count = lax.axis_size("row")
    col_count = lax.axis_size("col")
    row_index = lax.axis_index("row")
    col_index = lax.axis_index("col")
    own_count = support_views.shape[0]
    own_targets = target_views.shape[0]
    channels = support_views.shape[2]
    classes = support_labels.shape[1]
    own_support = choose_view(support_views, support_pick)
    own_target = choose_view(target_views, target_pick)
    support_pack = jnp.concatenate([own_support, self_maps(own_support)], axis=1)
    target_pack = jnp.concatenate([own_target, self_maps(own_target)], axis=1)
    row_pack = lax.all_gather(support_pack, "col", axis=0, tiled=True)
    column_pack, target_block = (
        lax.all_gather(support_pack, "row", axis=0, tiled=True),
        lax.all_gather(target_pack, "row", axis=0, tiled=True),
    )
    row_images = row_pack[:, :channels]
    row_maps = row_pack[:, channels:]
    column_images = column_pack[:, :channels]
    column_maps = column_pack[:, channels:]
    target_images = target_block[:, :channels]
    target_maps = target_block[:, channels:]
    row_start = row_index * col_count * own_count
    row_span = col_count * own_count
    support_tile = blocked_kernel(row_images, row_maps, column_images, column_maps)
    cross_tile = blocked_kernel(row_images, row_maps, target_images, target_maps)
    onehot_all = (target_labels[:, None] == jnp.arange(classes, dtype=jnp.int32)[None, :]).astype(
        jnp.float32
    ) - 1.0 / classes
    identity = jnp.eye(SUPPORT, dtype=jnp.float32)
    tiles, all_labels = (
        lax.all_gather(support_tile, ("row", "col"), axis=0, tiled=True),
        lax.all_gather(support_labels, ("row", "col"), axis=0, tiled=True),
    )
    support_kernel = assemble(tiles, row_count, col_count, own_count, own_count)
    trace_mean = jnp.trace(support_kernel) / SUPPORT
    factor = jnp.linalg.cholesky(support_kernel + ridge_scale * trace_mean * identity)
    alpha = solve_with(factor, all_labels)
    alpha_rows = lax.dynamic_slice_in_dim(alpha, row_start, row_span, 0)
    labels_here = column_of(onehot_all, col_index, row_count, col_count, own_targets)
    predicted = lax.psum(jnp.dot(cross_tile.T, alpha_rows, precision=highest), "row")
    error = predicted - labels_here
    adjoint_part, loss_sum = lax.psum(
        (jnp.dot(cross_tile, error, precision=highest), jnp.sum(error * error)), "col"
    )
    adjoint = lax.all_gather(adjoint_part, "row", axis=0, tiled=True)
    gamma = solve_with(factor, adjoint)
    intersection = jnp.sum(gamma * alpha)
    gamma_rows = lax.dynamic_slice_in_dim(gamma, row_start, row_span, 0)
    cross_weights = jnp.dot(alpha_rows, error.T, precision=highest)
    alpha_cols = column_of(alpha, col_index, row_count, col_count, own_count)
    row_ids = jnp.arange(row_span, dtype=jnp.int32)
    col_ids = jnp.arange(row_count * own_count, dtype=jnp.int32)
    on_diagonal = (
        (row_ids[:, None] // own_count == col_index)
        & (col_ids[None, :] // own_count == row_index)
        & (row_ids[:, None] % own_count == col_ids[None, :] % own_count)
    ).astype(jnp.float32)
    support_weights = (
        -jnp.dot(gamma_rows, alpha_cols.T, precision=highest)
        - ridge_scale * intersection / SUPPORT * on_diagonal
    )
    row_grad, row_map_grad, col_grad, col_map_grad = blocked_backward(
        row_images, row_maps, column_images, column_maps, support_weights, True
    )
    cross_grad, cross_map_grad, _, _ = blocked_backward(
        row_images, row_maps, target_images, target_maps, cross_weights, False
    )
    row_grad = row_grad + cross_grad
    row_map_grad = row_map_grad + cross_map_grad
    row_send = jnp.concatenate([row_grad, row_map_grad], axis=1)
    col_send = jnp.concatenate([col_grad, col_map_grad], axis=1)
    row_whole = lax.psum(row_send, "col")
    col_whole = lax.psum(col_send, "row")
    row_back = lax.dynamic_slice_in_dim(row_whole, col_index * own_count, own_count, 0)
    col_back = lax.dynamic_slice_in_dim(col_whole, row_index * own_count, own_count, 0)
    combined = row_back + col_back
    support_grad = combined[:, :channels] + self_back(own_support, combined[:, channels:])
    own_start = (row_index * col_count + col_index) * own_count
    label_grad = lax.dynamic_slice_in_dim(gamma, own_start, own_count, 0)
    return (support_grad, label_grad, 0.5 * loss_sum)


def solution(mesh):
    return jax.shard_map(
        body,
        mesh=mesh,
        in_specs=(
            P(("row", "col"), None, None, None),
            P(("row", "col")),
            P(("row", "col"), None, None, None),
            P(("row", "col")),
            P(("row", "col"), None),
            P(),
        ),
        out_specs=(P(("row", "col"), None, None), P(("row", "col"), None), P()),
        check_vma=False,
    )
```

profile of v0, /device:TPU:1, one launch (start us, length us, event | category | flops | bytes accessed | tf_op | source)
XLA Modules:
  0.0 1946.5 jit_solution(9639470266401859596)
XLA Ops:
  7.9 0.9 multiply_reduce_fusion.15
  9.6 0.9 multiply_reduce_fusion.14
  11.5 44.2 %all_gather.18 = f32[16,6,1024]{2,1,0:T(8,128)S(1)} all-gather(f32[1,6,1024]{2,1,0:T(8,128)S(1)} %copy.228), channel_id=1, replica_groups=mesh['row'=16,'col'=16] {'col'}, dimensions={0}, use_global_device_ids=true | all-gather | bytes 417792 | tf_op jit(solution)/shard_map/all_gather | solution.py:206
  55.7 28.3 %all_gather.19 = f32[16,6,1024]{2,1,0:T(8,128)S(1)} all-gather(f32[1,6,1024]{2,1,0:T(8,128)S(1)} %copy.228), channel_id=1, replica_groups=mesh['row'=16,'col'=16] {'row'}, dimensions={0}, use_global_device_ids=true | all-gather | bytes 417792 | tf_op jit(solution)/shard_map/all_gather | solution.py:208
  84.8 15.7 while.70
  85.4 0.8 multiply_multiply_fusion.25
  86.7 0.8 multiply_multiply_fusion.26
  87.9 0.9 multiply_reduce_fusion.26
  89.4 0.8 multiply_multiply_fusion.25
  90.6 0.8 multiply_multiply_fusion.26
  91.8 0.9 multiply_reduce_fusion.26
  93.3 0.8 multiply_multiply_fusion.25
  94.5 0.8 multiply_multiply_fusion.26
  95.8 0.9 multiply_reduce_fusion.26
  97.3 0.8 multiply_multiply_fusion.25
  98.5 0.8 multiply_multiply_fusion.26
  99.7 0.9 multiply_reduce_fusion.26
  100.7 648.1 %all_gather.20 = f32[4096,16]{1,0:T(8,128)} all-gather(f32[16,16]{1,0:T(8,128)S(1)} %copy.234), channel_id=1, replica_groups=mesh['row'=16,'col'=16] {'row','col'}, dimensions={0}, use_global_device_ids=true | all-gather | bytes 263168 | tf_op jit(solution)/shard_map/all_gather | solution.py:226
  748.8 3.0 copy.269
  751.8 2.0 copy.236
  753.8 2.6 reshape.1087
  756.4 1.3 select_reduce_fusion
  758.5 11.7 cholesky.49
  770.3 9.8 custom-call.17
  780.6 11.7 cholesky.103
  795.4 4.2 while.74
  796.0 1.4 dynamic-slice.16
  798.1 1.4 dynamic-slice.16
  799.6 19.9 %custom-call.27 = f32[2,128,128]{1,2,0:T(8,128)S(1)} custom-call(f32[2,128,128]{2,1,0:T(8,128)S(1)} %get-tuple-element.626), custom_call_target="InvertDiagBlocksLowerTriangular" | custom-call | tf_op jit(solution)/shard_map/triangular_solve/custom-call.4 | solution.py:176
  819.5 619.3 %all-gather = f32[256,1,10]{2,1,0:T(1,128)S(1)} all-gather(f32[1,1,10]{2,1,0:T(1,128)S(1)} %bitcast.419), channel_id=1, replica_groups=mesh['row'=16,'col'=16] {'row','col'}, dimensions={0}, use_global_device_ids=true | all-gather | bytes 10280 | tf_op jit(solution)/shard_map/all_gather | solution.py:227
  1441.0 41.5 %all_gather.21 = f32[16,6,1024]{2,1,0:T(8,128)S(1)} all-gather(f32[1,6,1024]{2,1,0:T(8,128)S(1)} %pad_maximum_fusion.2), channel_id=1, replica_groups=mesh['row'=16,'col'=16] {'row'}, dimensions={0}, use_global_device_ids=true | all-gather | bytes 417792 | tf_op jit(solution)/shard_map/all_gather | solution.py:209
  1482.9 15.8 while.71
  1483.6 0.8 multiply_multiply_fusion.27
  1484.8 0.8 multiply_multiply_fusion.28
  1486.0 0.9 multiply_reduce_fusion.27
  1487.5 0.8 multiply_multiply_fusion.27
  1488.7 0.8 multiply_multiply_fusion.28
  1489.9 0.9 multiply_reduce_fusion.27
  1491.4 0.8 multiply_multiply_fusion.27
  1492.7 0.8 multiply_multiply_fusion.28
  1493.9 0.9 multiply_reduce_fusion.27
  1495.4 0.8 multiply_multiply_fusion.27
  1496.6 0.8 multiply_multiply_fusion.28
  1497.8 0.9 multiply_reduce_fusion.27
  1498.9 27.1 %psum.35 = f32[16,10]{1,0:T(8,128)S(1)} all-reduce(f32[16,10]{1,0:T(8,128)S(1)} %fusion.103), channel_id=1, replica_groups=mesh['row'=16,'col'=16] {'row'}, use_global_device_ids=true, to_apply=%region_15.18 | all-reduce | flops 160 | bytes 1280 | tf_op jit(solution)/shard_map/psum | solution.py:235
  1527.4 33.7 %all-reduce.91 = (f32[16,10]{1,0:T(8,128)S(1)}, f32[]{:T(128)}) all-reduce(f32[16,10]{1,0:T(8,128)S(1)} %fusion.58, f32[]{:T(128)} %multiply_reduce_fusion.18), channel_id=1, replica_groups=mesh['row'=16,'col'=16] {'col'}, use_global_device_ids=true, to_apply=%region_16.19 | all-reduce | flops 161 | bytes 1288 | tf_op jit(solution)/shard_map/psum | solution.py:237
  1561.1 25.3 %all_gather.23 = f32[256,10]{1,0:T(8,128)S(1)} all-gather(f32[16,10]{1,0:T(8,128)S(1)} %get-tuple-element.1041), channel_id=1, replica_groups=mesh['row'=16,'col'=16] {'row'}, dimensions={0}, use_global_device_ids=true | all-gather | bytes 10880 | tf_op jit(solution)/shard_map/all_gather | solution.py:240
  1587.8 30.0 %while.73 = (s32[]{:T(128)}, f32[16,3,1024]{2,0,1:T(8,128)S(1)}, f32[16,3,1024]{2,0,1:T(8,128)S(1)}, f32[16,3,1024]{2,0,1:T(8,128)S(1)}, f32[4,4,3,1024]{3,1,2,0...) while((s32[]{:T(128)}, f32[16,3,1024]{2,0,1:T(8,128)S(1)}, ...), condition=%wide.region_39.42_spmd.clone, body=%wide.region_32.41_spmd.clone.sunk | while | flops 9070723 | bytes 30579320 | solution.py:155
  1588.8 0.8 multiply_multiply_fusion.33
  1590.0 0.8 multiply_multiply_fusion.34
  1597.4 0.8 multiply_multiply_fusion.34
  1604.8 0.8 multiply_multiply_fusion.34
  1612.2 0.8 multiply_multiply_fusion.34
  1619.8 31.6 %while.72 = (s32[]{:T(128)}, f32[16,3,1024]{2,0,1:T(8,128)S(1)}, f32[16,3,1024]{2,0,1:T(8,128)S(1)}, f32[4,4,3,1024]{3,1,0,2:T(4,128)S(1)}, f32[4,4,3,1024]{3,1,...) while((s32[]{:T(128)}, f32[16,3,1024]{2,0,1:T(8,128)S(1)}, ...), condition=%wide.region_31.34_spmd.clone, body=%wide.region_18.33_spmd.clone.sunk | while | flops 9758851 | bytes 33184396 | solution.py:155
  1620.7 0.8 multiply_multiply_fusion.29
  1622.0 0.8 multiply_multiply_fusion.30
  1629.8 0.8 multiply_multiply_fusion.30
  1637.6 0.8 multiply_multiply_fusion.30
  1644.3 0.8 multiply_multiply_fusion.29
  1645.5 0.8 multiply_multiply_fusion.30
  1652.5 0.8 pad_maximum_fusion.1
  1654.7 148.6 %all-reduce.95.cloned.1.call-done = f32[16,6,1024]{2,0,1:T(8,128)} async-done(((f32[16,6,1024]{2,0,1:T(8,128)}), f32[16,6,1024]{2,0,1:T(8,128)}) %all-reduce.95.cloned.1.call-update) | async-done | bytes 393232 | tf_op jit(solution)/shard_map/psum | solution.py:267
  1803.3 132.1 %all-reduce.97.cloned.1.call-done = f32[16,6,1024]{2,0,1:T(8,128)} async-done(((f32[16,6,1024]{2,0,1:T(8,128)}), f32[16,6,1024]{2,0,1:T(8,128)}) %all-reduce.97.cloned.1.call-update) | async-done | bytes 393232 | tf_op jit(solution)/shard_map/psum | solution.py:268
  1935.4 1.1 dynamic-slice_add_fusion
  (577 shorter events, 76.9 us)
Async XLA Ops:
  7.2 1796.2 %all-reduce.95.cloned.1.call-start = ((), (), s32[]{:S(2)}) async-start(), calls=%async_computation | async-start | bytes 786432 | tf_op jit(solution)/shard_map/psum | solution.py:267
  780.1 39.4 %copy-start.1 = (f32[1,10]{1,0:T(1,128)S(1)}, f32[1,10]{1,0:T(1,128)}, u32[]{:S(2)}) copy-start(f32[1,10]{1,0:T(1,128)} %param.22) | copy-start | bytes 124
  1482.9 43.1 %copy-start = (s32[256]{0:T(256)S(1)}, s32[256]{0:T(256)}, u32[]{:S(2)}) copy-start(s32[256]{0:T(256)} %param.23) | copy-start | bytes 3076
  1652.3 283.1 %all-reduce.97.cloned.1.call-start = ((), (), s32[]{:S(2)}) async-start(), calls=%async_computation.1 | async-start | bytes 786432 | tf_op jit(solution)/shard_map/psum | solution.py:268
Sparse Core Ops, SparseCore 0:
  1652.5 150.8 all-reduce.94
  1806.1 129.2 all-reduce.96
where the time goes:
time: 1950 us
  blocking collectives  1470 us (75%)
  waiting for transfers between devices  281 us (14%)
  other arithmetic  134 us (7%)
  local copies, waits for them, and re-layouts  36 us (2%)
  between operations  20.8 us (1%)
    all_gather x1, blocking collectives, body(): lax.all_gather(support_tile, ('row', 'col'), axis=0, tiled=True)  648 us
    all_gather x1, blocking collectives, body(): lax.all_gather(support_labels, ('row', 'col'), axis=0, tiled=True)  619 us
    psum x1, waiting for transfers between devices, body(): row_whole = lax.psum(row_send, 'col')  149 us
    psum x1, waiting for transfers between devices, body(): col_whole = lax.psum(col_send, 'row')  132 us
    all_gather x1, blocking collectives, body(): row_pack = lax.all_gather(support_pack, 'col', axis=0, tiled=True)  44.2 us
    all_gather x1, blocking collectives, body(): lax.all_gather(target_pack, 'row', axis=0, tiled=True)  41.5 us
  transfers between devices with their start and end apart: 2, of which 2 were waited for; matrix products, arithmetic and copies ran while one was open for 0% of the time, Pallas kernels for 0%

commit v1 on v0

v1 whole, which is shorter than its diff:
```python
import jax
import jax.numpy as jnp
import numpy as np
from jax import lax
from jax.experimental import pallas as pl
from jax.experimental.pallas import tpu as pltpu
from jax.sharding import PartitionSpec as P

PI = float(np.pi)
BIAS = 0.1
RIDGE = 0.1
GROUP = 16
PIX = 1024
SUPPORT = 256
CLASSES = 10
HIGHEST = lax.Precision.HIGHEST
F32 = jnp.float32
BF16 = jnp.bfloat16
ACOS = (
    1.570796251296997,
    -0.21459108591079712,
    0.08883588761091232,
    -0.04919743537902832,
    0.027762912213802338,
    -0.012003393843770027,
    0.0026117200031876564,
)


def inverse_schedule():
    low, high = RIDGE * 0.99, SUPPORT + 2 * RIDGE
    first = 2.0 / (low + high)
    error = (high - low) / (high + low)
    scales = []
    while error > 1e-7:
        scales.append(2.0 / (2.0 - error * error))
        error = error * error / (2.0 - error * error)
    return first, scales


FIRST_SCALE, SCALES = inverse_schedule()


def make_masks():
    lane = lax.broadcasted_iota(jnp.int32, (8, 128), 1)
    sub = lax.broadcasted_iota(jnp.int32, (8, 128), 0)
    col = lane & 31
    return dict(
        right=(col < 31).astype(F32),
        left=(col > 0).astype(F32),
        below=(sub < 7).astype(F32),
        above=(sub > 0).astype(F32),
        group=lane // 32,
        lane=lane,
    )


def box(x, m):
    h = (
        x
        + m["right"] * pltpu.roll(x, 127, x.ndim - 1)
        + m["left"] * pltpu.roll(x, 1, x.ndim - 1)
    )
    h0, h1, h2, h3 = (h[..., k, :, :] for k in range(4))
    above = pltpu.roll(h3, 1, h3.ndim - 2) * m["above"]
    below = pltpu.roll(h0, 7, h3.ndim - 2) * m["below"]
    a = h0 + h1
    b = h2 + h3
    return jnp.stack([above + a, a + h2, h1 + b, b + below], axis=-3)


def arc(c):
    c = jnp.clip(c, -1.0, 1.0)
    t = jnp.abs(c)
    w = 1.0 - t
    v = 1.0 + t
    q = w * lax.rsqrt(jnp.maximum(w, 1e-30))
    s = q * (v * lax.rsqrt(v))
    p = jnp.full_like(t, ACOS[-1])
    for a in ACOS[-2::-1]:
        p = p * t + a
    theta = q * p
    return s, jnp.where(c < 0, theta, PI - theta), c


def repeat_lanes(x, m):
    rolled = [x] + [pltpu.roll(x, 32 * i, x.ndim - 1) for i in (1, 2, 3)]
    out = []
    for k in range(4):
        y = rolled[0]
        for i in (1, 2, 3):
            y = jnp.where(m["group"] == ((k + i) % 4), rolled[i], y)
        out.append(y)
    return jnp.stack(out, axis=-3)


def pack_lanes(maps, m):
    rolled = [[x if i == 0 else pltpu.roll(x, 32 * i, x.ndim - 1) for i in range(4)] for x in maps]
    out = []
    for k in range(4):
        y = rolled[0][(0 - k) % 4]
        for j in (1, 2, 3):
            y = jnp.where(m["group"] == j, rolled[j][(j - k) % 4], y)
        out.append(y)
    return jnp.stack(out, axis=-3)


def merge_lanes(x, m):
    last = x.ndim - 1
    x = x + pltpu.roll(x, 64, last)
    x = x + pltpu.roll(x, 32, last)
    y = x[..., 0, :, :]
    for k in (1, 2, 3):
        y = jnp.where(m["group"] == k, x[..., k, :, :], y)
    return y


def self_maps(x, m):
    d = box((x[:, 0] * x[:, 0] + x[:, 1] * x[:, 1] + x[:, 2] * x[:, 2]) * (1.0 / 27.0), m) + BIAS
    maps = [d]
    for _ in range(2):
        d = box(d, m) * (1.0 / 9.0) + BIAS
        maps.append(d)
    return maps


def dot3(a, b):
    ah = a.astype(BF16)
    al = (a - ah.astype(F32)).astype(BF16)
    bh = b.astype(BF16)
    bl = (b - bh.astype(F32)).astype(BF16)
    d = lambda p, q: jnp.dot(p, q, preferred_element_type=F32)
    return d(ah, bh) + (d(ah, bl) + d(al, bh))


def dot6(a, b):
    return jnp.dot(a, b, precision=HIGHEST, preferred_element_type=F32)


def dot_nt(a, b):
    return lax.dot_general(
        a, b, (((1,), (1,)), ((), ())), precision=HIGHEST, preferred_element_type=F32
    )


def invert(a, identity):
    x = (SCALES[0] * FIRST_SCALE) * (2.0 * identity - FIRST_SCALE * a)
    count = len(SCALES)
    for i in range(1, count):
        mul = dot6 if i >= count - 2 else dot3
        x = SCALES[i] * mul(x, 2.0 * identity - mul(a, x))
    return x


def step_kernel(
    views_ref,
    pick_ref,
    target_views_ref,
    target_pick_ref,
    labels_ref,
    classes_ref,
    grad_out,
    label_out,
    loss_out,
    own,
    vraw,
    uraw,
    ui,
    um,
    vi,
    vm,
    phis,
    sines,
    partial,
    tile1,
    send_a,
    send_b,
    abuf,
    bbuf,
    side1,
    side2,
    wbuf,
    gsend,
    grecv,
    img_row_s,
    img_row_r,
    img_col_s,
    img_col_r,
    t1_s,
    t1_r,
    t2a_s,
    t2a_r,
    t2b_s,
    t2b_r,
    fin_s,
    fin_r,
):
    row = lax.axis_index("row")
    col = lax.axis_index("col")
    m = make_masks()

    def row_peer(d):
        return lax.rem(row + d, GROUP)

    def col_peer(d):
        return lax.rem(col + d, GROUP)

    def each_peer(body):
        def step(d, carry):
            body(d)
            return carry

        lax.fori_loop(1, GROUP, step, 0)

    def remote(src, dst, ssem, rsem, axis, peer):
        other = {"row": (peer, col), "col": (row, peer)}[axis]
        return pltpu.make_async_remote_copy(
            src_ref=src,
            dst_ref=dst,
            send_sem=ssem,
            recv_sem=rsem,
            device_id=other,
            device_id_type=pl.DeviceIdType.MESH,
        )

    def image_row(d, me, peer):
        return remote(own, vraw.at[me], img_row_s.at[d], img_row_r.at[me], "row", peer)

    def image_col(d, me, peer):
        return remote(own.at[pl.ds(0, 3)], uraw.at[me], img_col_s.at[d], img_col_r.at[me], "col", peer)

    def tile_row(d, me, peer):
        return remote(tile1.at[row], tile1.at[me], t1_s.at[d], t1_r.at[me], "row", peer)

    def block_a(d, me, peer):
        return remote(send_a, abuf.at[:, pl.ds(me * GROUP, GROUP)], t2a_s.at[d], t2a_r.at[me], "col", peer)

    def block_b(d, me, peer):
        return remote(send_b, bbuf.at[:, pl.ds(me * GROUP, GROUP)], t2b_s.at[d], t2b_r.at[me], "col", peer)

    def grad_col(d, me, peer):
        return remote(gsend.at[peer], grecv.at[me], fin_s.at[d], fin_r.at[me], "col", peer)

    def start_row(copy):
        each_peer(lambda d: copy(d, row, row_peer(d)).start())

    def start_col(copy):
        each_peer(lambda d: copy(d, col, col_peer(d)).start())

    def landed_row(copy):
        each_peer(lambda d: copy(d, row_peer(d), row_peer(d)).wait_recv())

    def landed_col(copy):
        each_peer(lambda d: copy(d, col_peer(d), col_peer(d)).wait_recv())

    barrier = pltpu.get_barrier_semaphore()

    def greet(d):
        pl.semaphore_signal(
            barrier, inc=1, device_id=(row_peer(d), col), device_id_type=pl.DeviceIdType.MESH
        )
        pl.semaphore_signal(
            barrier, inc=1, device_id=(row, col_peer(d)), device_id_type=pl.DeviceIdType.MESH
        )

    each_peer(greet)

    support = views_ref[0, pick_ref[0]]
    target = target_views_ref[0, target_pick_ref[0]]
    for k in range(8):
        own[0:3, k, :] = support[:, k * 128 : (k + 1) * 128]
        own[3:6, k, :] = target[:, k * 128 : (k + 1) * 128]
    own[6] = jnp.zeros((8, 128), F32)
    own[6, 0:1, 0:CLASSES] = labels_ref[...]
    pl.semaphore_wait(barrier, 2 * (GROUP - 1))
    start_row(image_row)
    start_col(image_col)
    vraw[row] = own[...]
    uraw[col] = own[0:3]
    landed_col(image_col)

    def prepare_rows(i, carry):
        us = pl.ds(i * 4, 4)
        x = repeat_lanes(uraw[us], m)
        ui[us] = x
        for l, d in enumerate(self_maps(x, m)):
            r = lax.rsqrt(d)
            um[us, l] = d * r * (1.0 / (9.0 * PI) if l < 2 else 1.0)
            um[us, 3 + l] = r
        return carry

    lax.fori_loop(0, 4, prepare_rows, 0)
    landed_row(image_row)
    for h in range(2):
        vs = pl.ds(4 * h, 4)
        x = pack_lanes(
            [vraw[pl.ds(8 * (j % 2) + 4 * h, 4), 3 * (j // 2) : 3 * (j // 2) + 3] for j in range(4)], m
        )
        vi[vs] = x * (1.0 / 27.0)
        for l, d in enumerate(self_maps(x, m)):
            r = lax.rsqrt(d)
            vm[vs, l] = d * r
            vm[vs, 3 + l] = r

    def forward(u, carry):
        k = box(ui[u, 0] * vi[:, 0] + ui[u, 1] * vi[:, 1] + ui[u, 2] * vi[:, 2], m) + BIAS
        for l in range(3):
            s, phi, c = arc(k * (um[u, 3 + l] * vm[:, 3 + l]))
            z = (s + phi * c) * (um[u, l] * vm[:, l])
            phis[l, u] = phi
            sines[l, u] = s * vm[:, l]
            if l < 2:
                k = box(z, m) + BIAS
        partial[u] = jnp.sum(jnp.sum(z, axis=1), axis=1)
        return carry

    lax.fori_loop(0, GROUP, forward, 0, unroll=2)

    shift = lax.rem(row, 8) * GROUP
    for j in range(4):
        acc = jnp.zeros((8, 128), F32)
        for u in range(GROUP):
            total = jnp.sum(jnp.where(m["group"] == j, partial[u], 0.0), axis=1, keepdims=True)
            acc = jnp.where(m["lane"] == shift + u, total, acc)
        tile1[row, 8 * j : 8 * j + 8] = acc * (1.0 / (PIX * PI))
    start_row(tile_row)

    def backward(u, carry):
        g = box(phis[2, u], m)
        sines[1, u] = g * sines[1, u]
        g = box(g * phis[1, u], m)
        sines[0, u] = g * sines[0, u]
        phis[0, u] = box(g * phis[0, u], m)
        return carry

    lax.fori_loop(0, 6, backward, 0, unroll=2)
    landed_row(tile_row)
    low = tile1[0]
    high = tile1[8]
    for i in range(1, 8):
        low = low + tile1[i]
        high = high + tile1[8 + i]
    send_a[0] = low[0:16]
    send_a[1] = high[0:16]
    send_b[0] = low[16:32]
    send_b[1] = high[16:32]
    for i in range(GROUP):
        send_a[2, i : i + 1, :] = vraw[i, 6, 0:1, :]
    start_col(block_a)
    start_col(block_b)
    abuf[:, pl.ds(col * GROUP, GROUP)] = send_a[...]
    bbuf[:, pl.ds(col * GROUP, GROUP)] = send_b[...]
    lax.fori_loop(6, GROUP, backward, 0, unroll=2)
    landed_col(block_a)

    natural = lambda ref, part: jnp.concatenate(
        [ref[part, pl.ds(i, GROUP, stride=GROUP), :] for i in range(GROUP)], axis=0
    )
    kss = jnp.concatenate([natural(abuf, 0), natural(abuf, 1)], axis=1)
    labels_t = jnp.transpose(natural(abuf, 2))[0:16]
    rows = lax.broadcasted_iota(jnp.int32, (256, 256), 0)
    cols = lax.broadcasted_iota(jnp.int32, (256, 256), 1)
    identity = (rows == cols).astype(F32)
    trace = jnp.sum(jnp.sum(kss * identity, axis=0, keepdims=True), axis=1, keepdims=True) * (
        1.0 / SUPPORT
    )
    scale = 1.0 / trace
    system = kss * scale + RIDGE * identity
    inverse = invert(system, identity)

    def solve(rhs_t):
        first = dot6(rhs_t, inverse)
        return (first + dot6(rhs_t - dot6(first, system), inverse)) * scale

    alpha_t = solve(labels_t)
    landed_col(block_b)
    kst_t = jnp.concatenate([natural(bbuf, 0), natural(bbuf, 1)], axis=1)
    class_row = lax.broadcasted_iota(jnp.int32, (16, 256), 0)
    wanted = jnp.where(
        class_row < CLASSES,
        (classes_ref[...] == class_row).astype(F32) - 1.0 / CLASSES,
        0.0,
    )
    error_t = dot_nt(alpha_t, kst_t) - wanted
    loss = jnp.sum(jnp.sum(error_t * error_t, axis=0, keepdims=True), axis=1, keepdims=True)
    loss_out[...] = 0.5 * loss
    gamma_t = solve(dot6(error_t, kst_t))
    inner = jnp.sum(jnp.sum(gamma_t * alpha_t, axis=0, keepdims=True), axis=1, keepdims=True)

    pad = jnp.zeros((80, 256), F32)
    side1[...] = jnp.transpose(jnp.concatenate([alpha_t, gamma_t, error_t, pad], axis=0))
    side2[...] = jnp.transpose(jnp.concatenate([-gamma_t, -alpha_t, alpha_t, pad], axis=0))
    mine = side1[pl.ds(col, GROUP, stride=GROUP), :]
    lane16 = lax.broadcasted_iota(jnp.int32, (16, 128), 1)
    sub16 = lax.broadcasted_iota(jnp.int32, (16, 128), 0)
    left = jnp.concatenate(
        [jnp.where(lane16 < 32, mine, 0.0), jnp.where(lane16 < 32, 0.0, mine)], axis=0
    )
    right = jnp.concatenate(
        [side2[pl.ds(row * GROUP, GROUP), :], jnp.zeros((112, 128), F32)], axis=0
    )
    weights = dot_nt(left, right)
    on_diagonal = ((sub16 == row) & (lane16 == col)).astype(F32)
    weights = jnp.concatenate(
        [weights[0:16] - (2.0 * RIDGE / SUPPORT) * inner * on_diagonal, weights[16:32]], axis=0
    )
    own_row = side1[pl.ds(row * GROUP + col, 1), :]
    label_out[...] = own_row[:, 16 : 16 + CLASSES]
    for u in range(GROUP):
        y = weights[0:8, u : u + 1] * jnp.ones((8, 128), F32)
        for j in (1, 2, 3):
            y = jnp.where(m["group"] == j, weights[8 * j : 8 * j + 8, u : u + 1], y)
        wbuf[u] = y

    step9 = 1.0 / (9.0 * PI)

    def contract(u, carry):
        h1 = h2 = h3 = g0 = g1 = g2 = None
        plus = lambda total, term: term if total is None else total + term
        for v in range(8):
            w = jnp.broadcast_to(wbuf[u, v : v + 1, :], (8, 128))
            h1 = plus(h1, w * sines[0, u, v])
            h2 = plus(h2, w * sines[1, u, v])
            h3 = plus(h3, w * sines[2, u, v])
            g = w * phis[0, u, v]
            g0 = plus(g0, g * vi[v, 0])
            g1 = plus(g1, g * vi[v, 1])
            g2 = plus(g2, g * vi[v, 2])
        each = 1.0 / (2.0 * PI * PIX)
        h3 = h3 * um[u, 5] * each
        h2 = h2 * um[u, 4] * (each * step9)
        h1 = h1 * um[u, 3] * (each * step9 * step9)
        back = h1 + box(h2 + box(h3, m) * (1.0 / 9.0), m) * (1.0 / 9.0)
        back = box(back, m) * (2.0 / 27.0)
        scale_image = 27.0 * step9**3 / (3.0 * PIX)
        x = ui[u]
        out = jnp.stack([g0, g1, g2], axis=0) * scale_image + back * x
        gsend[u] = merge_lanes(out, m)
        return carry

    lax.fori_loop(0, GROUP, contract, 0, unroll=2)
    start_col(grad_col)
    grecv[col] = gsend[col]
    landed_col(grad_col)
    total = grecv[0]
    for i in range(1, GROUP):
        total = total + grecv[i]
    for k in range(8):
        grad_out[0, :, k * 128 : (k + 1) * 128] = total[:, k, :]

    def sent(d):
        image_row(d, row, row_peer(d)).wait_send()
        image_col(d, col, col_peer(d)).wait_send()
        tile_row(d, row, row_peer(d)).wait_send()
        block_a(d, col, col_peer(d)).wait_send()
        block_b(d, col, col_peer(d)).wait_send()
        grad_col(d, col, col_peer(d)).wait_send()

    each_peer(sent)


def body(support_views, support_pick, target_views, target_pick, support_labels, target_labels):
    vmem = pl.BlockSpec(memory_space=pltpu.VMEM)
    smem = pl.BlockSpec(memory_space=pltpu.SMEM)
    buf = lambda *shape: pltpu.VMEM(shape, F32)
    grad, label_grad, loss = pl.pallas_call(
        step_kernel,
        name="kip_step",
        out_shape=(
            jax.ShapeDtypeStruct((1, 3, PIX), F32),
            jax.ShapeDtypeStruct((1, CLASSES), F32),
            jax.ShapeDtypeStruct((1, 1), F32),
        ),
        in_specs=[vmem, smem, vmem, smem, vmem, vmem],
        out_specs=(vmem, vmem, vmem),
        scratch_shapes=[
            buf(7, 8, 128),
            buf(GROUP, 7, 8, 128),
            buf(GROUP, 3, 8, 128),
            buf(GROUP, 3, 4, 8, 128),
            buf(GROUP, 6, 4, 8, 128),
            buf(8, 3, 4, 8, 128),
            buf(8, 6, 4, 8, 128),
            buf(3, GROUP, 8, 4, 8, 128),
            buf(3, GROUP, 8, 4, 8, 128),
            buf(GROUP, 8, 128),
            buf(GROUP, 32, 128),
            buf(3, GROUP, 128),
            buf(2, GROUP, 128),
            buf(3, 256, 128),
            buf(2, 256, 128),
            buf(256, 128),
            buf(256, 128),
            buf(GROUP, 8, 128),
            buf(GROUP, 3, 8, 128),
            buf(GROUP, 3, 8, 128),
        ]
        + [pltpu.SemaphoreType.DMA((GROUP,))] * 12,
        compiler_params=pltpu.CompilerParams(
            collective_id=0, has_side_effects=True, vmem_limit_bytes=56 << 20
        ),
    )(
        support_views,
        support_pick,
        target_views,
        target_pick,
        support_labels,
        target_labels.reshape(1, SUPPORT),
    )
    return grad, label_grad, loss.reshape(())


def solution(mesh):
    both = ("row", "col")
    return jax.shard_map(
        body,
        mesh=mesh,
        in_specs=(
            P(both, None, None, None),
            P(both),
            P(both, None, None, None),
            P(both),
            P(both, None),
            P(),
        ),
        out_specs=(P(both, None, None), P(both, None), P()),
        check_vma=False,
    )
```

time: 1950 us -> 87.1 us (0.04)
  the two profiles are of different devices: /device:TPU:1 before, /device:TPU:32 now
where the time goes in v1:
time: 87.1 us; the launch traced here: 86.8 us
  Pallas kernels  79.2 us (91%)
  local copies, waits for them, and re-layouts  3.97 us (5%)
  between operations  3.71 us (4%)
    pallas_call x1, Pallas kernels, body(): pl.pallas_call(step_kernel, name='kip_step', out_shape=(jax.ShapeDtypeStr...  79.2 us
    unnamed x8, local copies, waits for them, and re-layouts  3.97 us

profile of v1, /device:TPU:32, one launch (start us, length us, event | category | flops | bytes accessed | tf_op | source)
XLA Modules:
  0.0 86.8 jit_solution(5816540692647858754)
XLA Ops:
  1.9 0.0 copy-start
  1.9 1.5 %copy.9.views_ref = f32[1,4,3,1024]{3,2,1,0:T(4,128)} copy(f32[1,4,3,1024]{3,1,2,0:T(4,128)} %param.6) | data formatting | bytes 98304 | tf_op args[0]
  3.4 0.0 copy-done
  3.4 0.7 copy.10.target_views_ref
  4.1 79.2 %kip_step.1 = (f32[1,3,1024]{2,1,0:T(4,128)}, f32[1,10]{1,0:T(1,128)}, f32[1,1]{1,0:T(1,128)}) custom-call(f32[1,4,3,1024]{3,2,1,0:T(4,128)} %copy.9.views_ref, s32[1]{0:T(128)S(6)} %copy.14.pick_ref, f32[1,4,3,1024]{3,2,1,0:T(4,128)} %copy.10.target_views_ref, s32[1]{0:T(128)S(6)} %copy.15.target_pick_ref, f32[1,10]{1,0:T(1,128)} %labels_ref.1, ...), custom_call_target="tpu_custom_call" | custom-call | tf_op jit(solution)/shard_map/kip_step/pallas_call | solution.py:466
  83.2 0.0 copy-start.1
  83.2 1.3 %copy.11 = f32[1,3,1024]{2,0,1:T(1,128)} copy(f32[1,3,1024]{2,1,0:T(4,128)} %get-tuple-element.9) | data formatting | bytes 24576
  84.6 0.0 copy-done.1
  84.6 0.5 copy.16
Async XLA Ops:
  1.9 1.5 %copy-start = (f32[1,4,3,1024]{3,1,2,0:T(4,128)S(1)}, f32[1,4,3,1024]{3,1,2,0:T(4,128)}, u32[]{:S(2)}) copy-start(f32[1,4,3,1024]{3,1,2,0:T(4,128)} %param.8) | copy-start | bytes 147460
  83.2 1.3 %copy-start.1 = (f32[1,10]{1,0:T(1,128)S(1)}, f32[1,10]{1,0:T(1,128)}, u32[]{:S(2)}) copy-start(f32[1,10]{1,0:T(1,128)} %get-tuple-element.16) | copy-start | bytes 124

commit v2 on v1

v2 whole, which is shorter than its diff:
```python
import jax
import jax.numpy as jnp
import numpy as np
from jax import lax
from jax.experimental import pallas as pl
from jax.experimental.pallas import tpu as pltpu
from jax.sharding import PartitionSpec as P

PI = float(np.pi)
BIAS = 0.1
RIDGE = 0.1
GROUP = 16
PIX = 1024
SUPPORT = 256
CLASSES = 10
HIGHEST = lax.Precision.HIGHEST
F32 = jnp.float32
BF16 = jnp.bfloat16
ACOS = (
    1.570796251296997,
    -0.21459108591079712,
    0.08883588761091232,
    -0.04919743537902832,
    0.027762912213802338,
    -0.012003393843770027,
    0.0026117200031876564,
)


def inverse_schedule():
    low, high = RIDGE * 0.99, SUPPORT + 2 * RIDGE
    first = 2.0 / (low + high)
    error = (high - low) / (high + low)
    scales = []
    while error > 1e-7:
        scales.append(2.0 / (2.0 - error * error))
        error = error * error / (2.0 - error * error)
    return first, scales


FIRST_SCALE, SCALES = inverse_schedule()


def make_masks():
    lane = lax.broadcasted_iota(jnp.int32, (8, 128), 1)
    sub = lax.broadcasted_iota(jnp.int32, (8, 128), 0)
    col = lane & 31
    return dict(
        right=(col < 31).astype(F32),
        left=(col > 0).astype(F32),
        below=(sub < 7).astype(F32),
        above=(sub > 0).astype(F32),
        group=lane // 32,
        lane=lane,
    )


def box(x, m):
    h = (
        x
        + m["right"] * pltpu.roll(x, 127, x.ndim - 1)
        + m["left"] * pltpu.roll(x, 1, x.ndim - 1)
    )
    h0, h1, h2, h3 = (h[..., k, :, :] for k in range(4))
    above = pltpu.roll(h3, 1, h3.ndim - 2) * m["above"]
    below = pltpu.roll(h0, 7, h3.ndim - 2) * m["below"]
    a = h0 + h1
    b = h2 + h3
    return jnp.stack([above + a, a + h2, h1 + b, b + below], axis=-3)


def arc(c):
    t = jnp.abs(c)
    w = jnp.maximum(1.0 - t, 1e-30)
    v = 1.0 + t
    q = w * lax.rsqrt(w)
    s = q * (v * lax.rsqrt(v))
    p = jnp.full_like(t, ACOS[-1])
    for a in ACOS[-2::-1]:
        p = p * t + a
    theta = q * p
    return s, jnp.where(c < 0, theta, PI - theta)


def repeat_lanes(x, m):
    rolled = [x] + [pltpu.roll(x, 32 * i, x.ndim - 1) for i in (1, 2, 3)]
    out = []
    for k in range(4):
        y = rolled[0]
        for i in (1, 2, 3):
            y = jnp.where(m["group"] == ((k + i) % 4), rolled[i], y)
        out.append(y)
    return jnp.stack(out, axis=-3)


def pack_lanes(maps, m):
    rolled = [[x if i == 0 else pltpu.roll(x, 32 * i, x.ndim - 1) for i in range(4)] for x in maps]
    out = []
    for k in range(4):
        y = rolled[0][(0 - k) % 4]
        for j in (1, 2, 3):
            y = jnp.where(m["group"] == j, rolled[j][(j - k) % 4], y)
        out.append(y)
    return jnp.stack(out, axis=-3)


def merge_lanes(x, m):
    last = x.ndim - 1
    x = x + pltpu.roll(x, 64, last)
    x = x + pltpu.roll(x, 32, last)
    y = x[..., 0, :, :]
    for k in (1, 2, 3):
        y = jnp.where(m["group"] == k, x[..., k, :, :], y)
    return y


def self_maps(x, m):
    d = box((x[:, 0] * x[:, 0] + x[:, 1] * x[:, 1] + x[:, 2] * x[:, 2]) * (1.0 / 27.0), m) + BIAS
    maps = [d]
    for _ in range(2):
        d = box(d, m) * (1.0 / 9.0) + BIAS
        maps.append(d)
    return maps


def dot3(a, b):
    ah = a.astype(BF16)
    al = (a - ah.astype(F32)).astype(BF16)
    bh = b.astype(BF16)
    bl = (b - bh.astype(F32)).astype(BF16)
    d = lambda p, q: jnp.dot(p, q, preferred_element_type=F32)
    return d(ah, bh) + (d(ah, bl) + d(al, bh))


def dot6(a, b):
    return jnp.dot(a, b, precision=HIGHEST, preferred_element_type=F32)


def dot_nt(a, b):
    return lax.dot_general(
        a, b, (((1,), (1,)), ((), ())), precision=HIGHEST, preferred_element_type=F32
    )


def invert(a, identity):
    x = (SCALES[0] * FIRST_SCALE) * (2.0 * identity - FIRST_SCALE * a)
    count = len(SCALES)
    for i in range(1, count):
        mul = dot6 if i >= count - 2 else dot3
        x = SCALES[i] * mul(x, 2.0 * identity - mul(a, x))
    return x


def step_kernel(
    views_ref,
    pick_ref,
    target_views_ref,
    target_pick_ref,
    labels_ref,
    classes_ref,
    grad_out,
    label_out,
    loss_out,
    own,
    vraw,
    uraw,
    ui,
    um,
    vi,
    vm,
    phis,
    sines,
    partial,
    packed,
    send_a,
    send_b,
    abuf,
    bbuf,
    side1,
    side2,
    wbuf,
    gsend,
    grecv,
    img_row_s,
    img_row_r,
    img_col_s,
    img_col_r,
    t1_s,
    t1_r,
    t2a_s,
    t2a_r,
    t2b_s,
    t2b_r,
    fin_s,
    fin_r,
):
    row = lax.axis_index("row")
    col = lax.axis_index("col")
    sibling = row + 1 - 2 * lax.rem(row, 2)
    m = make_masks()

    def row_peer(d):
        return lax.rem(row + d, GROUP)

    def col_peer(d):
        return lax.rem(col + d, GROUP)

    def same_core(d):
        return lax.rem(row + 2 * d, GROUP)

    def along_z(d):
        return (col // 4) * 4 + lax.rem(col + d, 4)

    def along_x(d):
        return lax.rem(col + 4 * d, GROUP)

    def loop(low, high, body):
        def step(d, carry):
            body(d)
            return carry

        lax.fori_loop(low, high, step, 0)

    def remote(src, dst, ssem, rsem, device):
        return pltpu.make_async_remote_copy(
            src_ref=src,
            dst_ref=dst,
            send_sem=ssem,
            recv_sem=rsem,
            device_id=device,
            device_id_type=pl.DeviceIdType.MESH,
        )

    def image_row(src, k, slot, peer):
        return remote(src, vraw.at[slot], img_row_s.at[k], img_row_r.at[slot], (peer, col))

    def image_col(src, k, slot, peer):
        return remote(src, uraw.at[slot], img_col_s.at[k], img_col_r.at[slot], (row, peer))

    def tile_col(d, slot, peer):
        return remote(packed.at[col], packed.at[slot], t1_s.at[d], t1_r.at[slot], (row, peer))

    def block_a(d, slot, peer):
        return remote(
            send_a, abuf.at[:, pl.ds(slot * GROUP, GROUP)], t2a_s.at[d], t2a_r.at[slot], (peer, col)
        )

    def block_b(d, slot, peer):
        return remote(
            send_b, bbuf.at[:, pl.ds(slot * GROUP, GROUP)], t2b_s.at[d], t2b_r.at[slot], (peer, col)
        )

    def grad_col(d, slot, peer):
        return remote(gsend.at[peer], grecv.at[slot], fin_s.at[d], fin_r.at[slot], (row, peer))

    barrier = pltpu.get_barrier_semaphore()

    def greet(d):
        pl.semaphore_signal(
            barrier, inc=1, device_id=(row, col_peer(d)), device_id_type=pl.DeviceIdType.MESH
        )
        pl.semaphore_signal(
            barrier, inc=1, device_id=(row_peer(d), col), device_id_type=pl.DeviceIdType.MESH
        )

    loop(1, GROUP, greet)

    for c in range(3):
        support = views_ref[0, c, pl.ds(pick_ref[0], 1), :]
        target = target_views_ref[0, c, pl.ds(target_pick_ref[0], 1), :]
        for k in range(8):
            own[c, k : k + 1, :] = support[:, k * 128 : (k + 1) * 128]
            own[3 + c, k : k + 1, :] = target[:, k * 128 : (k + 1) * 128]
    pl.semaphore_wait(barrier, 2 * (GROUP - 1))
    mine = own.at[pl.ds(0, 3)]
    loop(1, 8, lambda d: image_row(own, d, row, same_core(d)).start())
    loop(1, 4, lambda d: image_col(mine, d, col, along_z(d)).start())
    image_row(own, 0, row, sibling).start()
    loop(1, 4, lambda d: image_col(mine, 3 + d, col, along_x(d)).start())
    vraw[row] = own[...]
    uraw[col] = own[0:3]

    def forward_x(d):
        slot = along_z(d)
        image_col(mine, 0, slot, slot).wait_recv()
        loop(1, 4, lambda e: image_col(uraw.at[slot], 3 + 3 * d + e, slot, along_x(e)).start())

    loop(1, 4, forward_x)

    def forward_core(d):
        slot = same_core(d)
        image_row(own, 0, slot, slot).wait_recv()
        image_row(vraw.at[slot], 7 + d, slot, sibling).start()

    loop(1, 8, forward_core)

    def landed_x(e):
        loop(0, 4, lambda d: image_col(mine, 0, (along_x(e) // 4) * 4 + d, col).wait_recv())

    loop(1, 4, landed_x)

    def prepare_rows(i):
        us = pl.ds(i * 4, 4)
        x = repeat_lanes(uraw[us], m)
        ui[us] = x
        for l, d in enumerate(self_maps(x, m)):
            r = lax.rsqrt(d)
            um[us, l] = d * r * (1.0 / (9.0 * PI) if l < 2 else 1.0)
            um[us, 3 + l] = r

    loop(0, 4, prepare_rows)
    loop(0, 8, lambda d: image_row(own, 0, 2 * d + lax.rem(row + 1, 2), row).wait_recv())
    for h in range(2):
        vs = pl.ds(4 * h, 4)
        x = pack_lanes(
            [vraw[pl.ds(8 * (j % 2) + 4 * h, 4), 3 * (j // 2) : 3 * (j // 2) + 3] for j in range(4)], m
        )
        vi[vs] = x * (1.0 / 27.0)
        for l, d in enumerate(self_maps(x, m)):
            r = lax.rsqrt(d)
            vm[vs, l] = d * r
            vm[vs, 3 + l] = r

    def forward(u, carry):
        k = box(ui[u, 0] * vi[:, 0] + ui[u, 1] * vi[:, 1] + ui[u, 2] * vi[:, 2], m) + BIAS
        for l in range(3):
            y = k * um[u, 3 + l]
            s, phi = arc(y * vm[:, 3 + l])
            s = s * vm[:, l]
            z = (s + phi * y) * um[u, l]
            phis[l, u] = phi
            sines[l, u] = s
            if l < 2:
                k = box(z, m) + BIAS
        total = jnp.sum(jnp.sum(z, axis=1), axis=1)
        for v in range(8):
            partial[v, pl.ds(u, 1), :] = total[v : v + 1]
        return carry

    lax.fori_loop(0, GROUP, forward, 0, unroll=2)

    tile = jnp.zeros((8, 128), F32)
    for half in range(2):
        for j in range(4):
            for v in range(8):
                part = partial[v, 8 * half : 8 * half + 8, :]
                total = jnp.sum(jnp.where(m["group"] == j, part, 0.0), axis=1, keepdims=True)
                lane = 16 * (2 * (j // 2) + half) + 8 * (j % 2) + v
                tile = jnp.where(m["lane"] == lane, total, tile)
    packed[col] = tile * (1.0 / (PIX * PI))
    packed[col, 0:1, 64 : 64 + CLASSES] = labels_ref[...]
    loop(1, GROUP, lambda d: tile_col(d, col, col_peer(d)).start())

    def backward(u, carry):
        g = box(phis[2, u], m)
        sines[1, u] = g * sines[1, u]
        g = box(g * phis[1, u], m)
        sines[0, u] = g * sines[0, u]
        phis[0, u] = box(g * phis[0, u], m)
        return carry

    lax.fori_loop(0, 6, backward, 0, unroll=2)
    loop(1, GROUP, lambda d: tile_col(d, col_peer(d), col).wait_recv())
    slot_of = m["lane"] // 16
    for kind, block in ((0, send_a), (1, send_b)):
        for half in range(2):
            for h in range(2):
                acc = jnp.zeros((8, 128), F32)
                for c in range(8):
                    moved = packed[8 * h + c]
                    turn = (c - 2 * kind - half) % 8
                    if turn:
                        moved = pltpu.roll(moved, 16 * turn, 1)
                    acc = jnp.where(slot_of == c, moved, acc)
                block[h, 8 * half : 8 * half + 8, :] = acc
    for c in range(GROUP):
        send_b[2, c : c + 1, :] = jnp.where(
            m["lane"][0:1] < CLASSES, pltpu.roll(packed[c, 0:1, :], 64, 1), 0.0
        )
    loop(1, GROUP, lambda d: block_a(d, row, row_peer(d)).start())
    loop(1, GROUP, lambda d: block_b(d, row, row_peer(d)).start())
    abuf[:, pl.ds(row * GROUP, GROUP)] = send_a[...]
    bbuf[:, pl.ds(row * GROUP, GROUP)] = send_b[...]
    lax.fori_loop(6, GROUP, backward, 0, unroll=2)

    rows = lax.broadcasted_iota(jnp.int32, (256, 256), 0)
    cols = lax.broadcasted_iota(jnp.int32, (256, 256), 1)
    identity = (rows == cols).astype(F32)
    permute = (rows == lax.rem(cols, GROUP) * GROUP + cols // GROUP).astype(BF16)
    class_row = lax.broadcasted_iota(jnp.int32, (16, 256), 0)
    onehot = (classes_ref[...] == class_row).astype(BF16)
    wanted = jnp.dot(onehot, permute, preferred_element_type=F32) - jnp.where(
        class_row < CLASSES, 1.0 / CLASSES, 0.0
    )
    loop(1, GROUP, lambda d: block_a(d, row_peer(d), row).wait_recv())
    ordered = lambda ref, part: jnp.concatenate(
        [ref[part, pl.ds(i, GROUP, stride=GROUP), :] for i in range(GROUP)], axis=0
    )
    kss = jnp.concatenate([ordered(abuf, 0), ordered(abuf, 1)], axis=1)
    trace = jnp.sum(jnp.sum(kss * identity, axis=0, keepdims=True), axis=1, keepdims=True) * (
        1.0 / SUPPORT
    )
    scale = 1.0 / trace
    system = kss * scale + RIDGE * identity
    inverse = invert(system, identity)

    def solve(rhs_t):
        first = dot6(rhs_t, inverse)
        return (first + dot6(rhs_t - dot6(first, system), inverse)) * scale

    loop(1, GROUP, lambda d: block_b(d, row_peer(d), row).wait_recv())
    labels_t = jnp.transpose(ordered(bbuf, 2))[0:16]
    kst = jnp.concatenate([ordered(bbuf, 0), ordered(bbuf, 1)], axis=1)
    alpha_t = solve(labels_t)
    error_t = dot6(alpha_t, kst) - wanted
    loss = jnp.sum(jnp.sum(error_t * error_t, axis=0, keepdims=True), axis=1, keepdims=True)
    loss_out[...] = 0.5 * loss
    gamma_t = solve(dot_nt(error_t, kst))
    inner = jnp.sum(jnp.sum(gamma_t * alpha_t, axis=0, keepdims=True), axis=1, keepdims=True)

    pad = jnp.zeros((80, 256), F32)
    side1[...] = jnp.transpose(jnp.concatenate([alpha_t, gamma_t, error_t, pad], axis=0))
    side2[...] = jnp.transpose(jnp.concatenate([-gamma_t, -alpha_t, alpha_t, pad], axis=0))
    column = side1[pl.ds(col * GROUP, GROUP), :]
    lane16 = lax.broadcasted_iota(jnp.int32, (16, 128), 1)
    sub16 = lax.broadcasted_iota(jnp.int32, (16, 128), 0)
    left = jnp.concatenate(
        [jnp.where(lane16 < 32, column, 0.0), jnp.where(lane16 < 32, 0.0, column)], axis=0
    )
    right = jnp.concatenate(
        [side2[pl.ds(row, GROUP, stride=GROUP), :], jnp.zeros((112, 128), F32)], axis=0
    )
    weights = dot_nt(left, right)
    on_diagonal = ((sub16 == row) & (lane16 == col)).astype(F32)
    weights = jnp.concatenate(
        [weights[0:16] - (2.0 * RIDGE / SUPPORT) * inner * on_diagonal, weights[16:32]], axis=0
    )
    own_row = side1[pl.ds(col * GROUP + row, 1), :]
    label_out[...] = own_row[:, 16 : 16 + CLASSES]
    for u in range(GROUP):
        y = weights[0:8, u : u + 1] * jnp.ones((8, 128), F32)
        for j in (1, 2, 3):
            y = jnp.where(m["group"] == j, weights[8 * j : 8 * j + 8, u : u + 1], y)
        wbuf[u] = y

    step9 = 1.0 / (9.0 * PI)
    each = 1.0 / (2.0 * PI * PIX)
    scale_image = 27.0 * step9**3 / (3.0 * PIX)

    def contract(u):
        sums = None
        for v in range(8):
            w = jnp.broadcast_to(wbuf[u, v : v + 1, :], (8, 128))
            g = w * phis[0, u, v]
            terms = [w * sines[l, u, v] for l in range(3)] + [g * vi[v, c] for c in range(3)]
            sums = terms if sums is None else [a + b for a, b in zip(sums, terms)]
        h = [sums[l] * um[u, 3 + l] * (each * step9 ** (2 - l)) for l in range(3)]
        return h, jnp.stack(sums[3:], axis=0) * scale_image, ui[u]

    def batch(b, last):
        us = [col_peer(1 + 4 * b + i) for i in range(4)]
        parts = [contract(u) for u in us]
        h1, h2, h3 = (jnp.stack([p[0][l] for p in parts], axis=0) for l in range(3))
        back = h1 + box(h2 + box(h3, m) * (1.0 / 9.0), m) * (1.0 / 9.0)
        back = box(back, m) * (2.0 / 27.0)
        image = jnp.stack([p[1] for p in parts], axis=0)
        x = jnp.stack([p[2] for p in parts], axis=0)
        out = merge_lanes(image + back[:, None] * x, m)
        for i, u in enumerate(us):
            if last and i == 3:
                grecv[col] = out[i]
            else:
                gsend[u] = out[i]
                grad_col(1 + 4 * b + i, col, u).start()

    loop(0, 3, lambda b: batch(b, False))
    batch(3, True)

    def sent_row(d):
        block_a(d, row, row_peer(d)).wait_send()
        block_b(d, row, row_peer(d)).wait_send()
        image_col(mine, d, col, col_peer(d)).wait_send()
        tile_col(d, col, col_peer(d)).wait_send()
        grad_col(d, col, col_peer(d)).wait_send()

    loop(1, GROUP, sent_row)
    loop(0, GROUP - 1, lambda k: image_row(own, k, row, sibling).wait_send())
    loop(1, GROUP, lambda d: grad_col(d, col_peer(d), col).wait_recv())
    total = grecv[0]
    for i in range(1, GROUP):
        total = total + grecv[i]
    for c in range(3):
        for k in range(8):
            grad_out[c, 0:1, k * 128 : (k + 1) * 128] = total[c, k : k + 1, :]


def body(support_views, support_pick, target_views, target_pick, support_labels, target_labels):
    vmem = pl.BlockSpec(memory_space=pltpu.VMEM)
    smem = pl.BlockSpec(memory_space=pltpu.SMEM)
    buf = lambda *shape: pltpu.VMEM(shape, F32)
    grad, label_grad, loss = pl.pallas_call(
        step_kernel,
        name="kip_step",
        out_shape=(
            jax.ShapeDtypeStruct((3, 1, PIX), F32),
            jax.ShapeDtypeStruct((1, CLASSES), F32),
            jax.ShapeDtypeStruct((1, 1), F32),
        ),
        in_specs=[vmem, smem, vmem, smem, vmem, vmem],
        out_specs=(vmem, vmem, vmem),
        scratch_shapes=[
            buf(6, 8, 128),
            buf(GROUP, 6, 8, 128),
            buf(GROUP, 3, 8, 128),
            buf(GROUP, 3, 4, 8, 128),
            buf(GROUP, 6, 4, 8, 128),
            buf(8, 3, 4, 8, 128),
            buf(8, 6, 4, 8, 128),
            buf(3, GROUP, 8, 4, 8, 128),
            buf(3, GROUP, 8, 4, 8, 128),
            buf(8, GROUP, 128),
            buf(GROUP, 8, 128),
            buf(2, GROUP, 128),
            buf(3, GROUP, 128),
            buf(2, 256, 128),
            buf(3, 256, 128),
            buf(256, 128),
            buf(256, 128),
            buf(GROUP, 8, 128),
            buf(GROUP, 3, 8, 128),
            buf(GROUP, 3, 8, 128),
        ]
        + [pltpu.SemaphoreType.DMA((GROUP,))] * 12,
        compiler_params=pltpu.CompilerParams(
            collective_id=0, has_side_effects=True, vmem_limit_bytes=56 << 20
        ),
    )(
        jnp.transpose(support_views, (0, 2, 1, 3)),
        support_pick,
        jnp.transpose(target_views, (0, 2, 1, 3)),
        target_pick,
        support_labels,
        target_labels.reshape(1, SUPPORT),
    )
    return jnp.transpose(grad, (1, 0, 2)), label_grad, loss.reshape(())


def solution(mesh):
    both = ("row", "col")
    return jax.shard_map(
        body,
        mesh=mesh,
        in_specs=(
            P(both, None, None, None),
            P(both),
            P(both, None, None, None),
            P(both),
            P(both, None),
            P(),
        ),
        out_specs=(P(both, None, None), P(both, None), P()),
        check_vma=False,
    )
```

time: 87.1 us -> 72.4 us (0.83)
  the two profiles are of different devices: /device:TPU:32 before, /device:TPU:1 now
where the time goes in v2:
time: 72.4 us; the launch traced here: 72.1 us
  Pallas kernels  66.6 us (92%)
  between operations  3.68 us (5%)
  local copies, waits for them, and re-layouts  1.82 us (3%)
    pallas_call x1, Pallas kernels, body(): pl.pallas_call(step_kernel, name='kip_step', out_shape=(jax.ShapeDtypeStr...  66.6 us
    unnamed x4, local copies, waits for them, and re-layouts  1.82 us

profile of v2, /device:TPU:1, one launch (start us, length us, event | category | flops | bytes accessed | tf_op | source)
XLA Modules:
  0.0 72.1 jit_solution(12439916877600144685)
XLA Ops:
  1.9 66.6 %kip_step.1 = (f32[3,1,1024]{2,1,0:T(1,128)}, f32[1,10]{1,0:T(1,128)}, f32[1,1]{1,0:T(1,128)}) custom-call(f32[1,3,4,1024]{3,2,1,0:T(4,128)} %bitcast.5, s32[1]{0:T(128)S(6)} %copy.12.pick_ref, f32[1,3,4,1024]{3,2,1,0:T(4,128)} %bitcast.6, s32[1]{0:T(128)S(6)} %copy.13.target_pick_ref, f32[1,10]{1,0:T(1,128)} %labels_ref.1, s32[1,256]{1,0:T(1,128)} %bitcast.8), custom_call_target="tpu_custom_call" | custom-call | tf_op jit(solution)/shard_map/kip_step/pallas_call | solution.py:501
  68.6 0.0 copy-start
  68.6 1.3 %copy.14 = f32[1,3,1024]{2,0,1:T(1,128)} copy(f32[1,3,1024]{2,0,1:T(1,128)} %bitcast.7) | data formatting | bytes 24576
  69.9 0.0 copy-done
  69.9 0.5 copy.15
Async XLA Ops:
  68.6 1.3 %copy-start = (f32[1,10]{1,0:T(1,128)S(1)}, f32[1,10]{1,0:T(1,128)}, u32[]{:S(2)}) copy-start(f32[1,10]{1,0:T(1,128)} %get-tuple-element.13) | copy-start | bytes 124

commit v3 on v2

--- a/solution.py
+++ b/solution.py
@@ -32,13 +32,15 @@
     first = 2.0 / (low + high)
     error = (high - low) / (high + low)
     scales = []
-    while error > 1e-7:
+    while error > 2e-4:
         scales.append(2.0 / (2.0 - error * error))
         error = error * error / (2.0 - error * error)
     return first, scales
 
 
 FIRST_SCALE, SCALES = inverse_schedule()
+BEFORE = 10
+assert GROUP - BEFORE <= 2 * (len(SCALES) - 1)
 
 
 def make_masks():
@@ -142,12 +144,15 @@
     )
 
 
-def invert(a, identity):
+def invert(a, identity, beside):
     x = (SCALES[0] * FIRST_SCALE) * (2.0 * identity - FIRST_SCALE * a)
     count = len(SCALES)
     for i in range(1, count):
-        mul = dot6 if i >= count - 2 else dot3
-        x = SCALES[i] * mul(x, 2.0 * identity - mul(a, x))
+        mul = dot6 if i == count - 1 else dot3
+        product = mul(a, x)
+        beside(2 * i - 2)
+        x = SCALES[i] * mul(x, 2.0 * identity - product)
+        beside(2 * i - 1)
     return x
 
 
@@ -172,21 +177,27 @@
     sines,
     partial,
     packed,
+    packed_b,
     send_a,
     send_b,
     abuf,
     bbuf,
     side1,
     side2,
+    wleft,
     wbuf,
     gsend,
     grecv,
     img_row_s,
     img_row_r,
+    img_tgt_s,
+    img_tgt_r,
     img_col_s,
     img_col_r,
     t1_s,
     t1_r,
+    t1b_s,
+    t1b_r,
     t2a_s,
     t2a_r,
     t2b_s,
@@ -194,25 +205,20 @@
     fin_s,
     fin_r,
 ):
-    row = lax.axis_index("row")
-    col = lax.axis_index("col")
-    sibling = row + 1 - 2 * lax.rem(row, 2)
+    mesh_row = lax.axis_index("row")
+    mesh_col = lax.axis_index("col")
+    row = (mesh_col // 4) * 4 + mesh_row // 4
+    col = lax.rem(mesh_col, 4) * 4 + lax.rem(mesh_row, 4)
     m = make_masks()
+
+    def device(r, c):
+        return (lax.rem(r, 4) * 4 + lax.rem(c, 4), (r // 4) * 4 + c // 4)
 
     def row_peer(d):
         return lax.rem(row + d, GROUP)
 
     def col_peer(d):
         return lax.rem(col + d, GROUP)
-
-    def same_core(d):
-        return lax.rem(row + 2 * d, GROUP)
-
-    def along_z(d):
-        return (col // 4) * 4 + lax.rem(col + d, 4)
-
-    def along_x(d):
-        return lax.rem(col + 4 * d, GROUP)
 
     def loop(low, high, body):
         def step(d, carry):
@@ -220,6 +226,14 @@
             return carry
 
         lax.fori_loop(low, high, step, 0)
+
+    def far_first(start):
+        def pair(k):
+            start(8 + k)
+            start(7 - k)
+
+        loop(0, 7, pair)
+        start(15)
 
     def remote(src, dst, ssem, rsem, device):
         return pltpu.make_async_remote_copy(
@@ -231,36 +245,49 @@
             device_id_type=pl.DeviceIdType.MESH,
         )
 
-    def image_row(src, k, slot, peer):
-        return remote(src, vraw.at[slot], img_row_s.at[k], img_row_r.at[slot], (peer, col))
-
-    def image_col(src, k, slot, peer):
-        return remote(src, uraw.at[slot], img_col_s.at[k], img_col_r.at[slot], (row, peer))
+    mine = own.at[pl.ds(0, 3)]
+    mine_tgt = own.at[pl.ds(3, 3)]
+
+    def image_row(d, slot, peer):
+        return remote(
+            mine, vraw.at[slot, pl.ds(0, 3)], img_row_s.at[d], img_row_r.at[slot], device(peer, col)
+        )
+
+    def image_tgt(d, slot, peer):
+        return remote(
+            mine_tgt, vraw.at[slot, pl.ds(3, 3)], img_tgt_s.at[d], img_tgt_r.at[slot], device(peer, col)
+        )
+
+    def image_col(d, slot, peer):
+        return remote(mine, uraw.at[slot], img_col_s.at[d], img_col_r.at[slot], device(row, peer))
 
     def tile_col(d, slot, peer):
-        return remote(packed.at[col], packed.at[slot], t1_s.at[d], t1_r.at[slot], (row, peer))
+        return remote(packed.at[col], packed.at[slot], t1_s.at[d], t1_r.at[slot], device(row, peer))
+
+    def tile_col_b(d, slot, peer):
+        return remote(packed_b.at[col], packed_b.at[slot], t1b_s.at[d], t1b_r.at[slot], device(row, peer))
 
     def block_a(d, slot, peer):
         return remote(
-            send_a, abuf.at[:, pl.ds(slot * GROUP, GROUP)], t2a_s.at[d], t2a_r.at[slot], (peer, col)
+            send_a, abuf.at[:, pl.ds(slot * GROUP, GROUP)], t2a_s.at[d], t2a_r.at[slot], device(peer, col)
         )
 
     def block_b(d, slot, peer):
         return remote(
-            send_b, bbuf.at[:, pl.ds(slot * GROUP, GROUP)], t2b_s.at[d], t2b_r.at[slot], (peer, col)
+            send_b, bbuf.at[:, pl.ds(slot * GROUP, GROUP)], t2b_s.at[d], t2b_r.at[slot], device(peer, col)
         )
 
     def grad_col(d, slot, peer):
-        return remote(gsend.at[peer], grecv.at[slot], fin_s.at[d], fin_r.at[slot], (row, peer))
+        return remote(gsend.at[peer], grecv.at[slot], fin_s.at[d], fin_r.at[slot], device(row, peer))
 
     barrier = pltpu.get_barrier_semaphore()
 
     def greet(d):
         pl.semaphore_signal(
-            barrier, inc=1, device_id=(row, col_peer(d)), device_id_type=pl.DeviceIdType.MESH
+            barrier, inc=1, device_id=device(row, col_peer(d)), device_id_type=pl.DeviceIdType.MESH
         )
         pl.semaphore_signal(
-            barrier, inc=1, device_id=(row_peer(d), col), device_id_type=pl.DeviceIdType.MESH
+            barrier, inc=1, device_id=device(row_peer(d), col), device_id_type=pl.DeviceIdType.MESH
         )
 
     loop(1, GROUP, greet)
@@ -272,32 +299,12 @@
             own[c, k : k + 1, :] = support[:, k * 128 : (k + 1) * 128]
             own[3 + c, k : k + 1, :] = target[:, k * 128 : (k + 1) * 128]
     pl.semaphore_wait(barrier, 2 * (GROUP - 1))
-    mine = own.at[pl.ds(0, 3)]
-    loop(1, 8, lambda d: image_row(own, d, row, same_core(d)).start())
-    loop(1, 4, lambda d: image_col(mine, d, col, along_z(d)).start())
-    image_row(own, 0, row, sibling).start()
-    loop(1, 4, lambda d: image_col(mine, 3 + d, col, along_x(d)).start())
+    far_first(lambda d: image_col(d, col, col_peer(d)).start())
+    far_first(lambda d: image_row(d, row, row_peer(d)).start())
+    far_first(lambda d: image_tgt(d, row, row_peer(d)).start())
     vraw[row] = own[...]
     uraw[col] = own[0:3]
-
-    def forward_x(d):
-        slot = along_z(d)
-        image_col(mine, 0, slot, slot).wait_recv()
-        loop(1, 4, lambda e: image_col(uraw.at[slot], 3 + 3 * d + e, slot, along_x(e)).start())
-
-    loop(1, 4, forward_x)
-
-    def forward_core(d):
-        slot = same_core(d)
-        image_row(own, 0, slot, slot).wait_recv()
-        image_row(vraw.at[slot], 7 + d, slot, sibling).start()
-
-    loop(1, 8, forward_core)
-
-    def landed_x(e):
-        loop(0, 4, lambda d: image_col(mine, 0, (along_x(e) // 4) * 4 + d, col).wait_recv())
-
-    loop(1, 4, landed_x)
+    loop(1, GROUP, lambda d: image_col(d, col_peer(d), col).wait_recv())
 
     def prepare_rows(i):
         us = pl.ds(i * 4, 4)
@@ -309,47 +316,61 @@
             um[us, 3 + l] = r
 
     loop(0, 4, prepare_rows)
-    loop(0, 8, lambda d: image_row(own, 0, 2 * d + lax.rem(row + 1, 2), row).wait_recv())
-    for h in range(2):
-        vs = pl.ds(4 * h, 4)
-        x = pack_lanes(
-            [vraw[pl.ds(8 * (j % 2) + 4 * h, 4), 3 * (j // 2) : 3 * (j // 2) + 3] for j in range(4)], m
-        )
+
+    def prepare_columns(kind):
+        vs = slice(4 * kind, 4 * kind + 4)
+        x = pack_lanes([vraw[4 * j : 4 * j + 4, 3 * kind : 3 * kind + 3] for j in range(4)], m)
         vi[vs] = x * (1.0 / 27.0)
         for l, d in enumerate(self_maps(x, m)):
             r = lax.rsqrt(d)
             vm[vs, l] = d * r
             vm[vs, 3 + l] = r
 
-    def forward(u, carry):
-        k = box(ui[u, 0] * vi[:, 0] + ui[u, 1] * vi[:, 1] + ui[u, 2] * vi[:, 2], m) + BIAS
-        for l in range(3):
-            y = k * um[u, 3 + l]
-            s, phi = arc(y * vm[:, 3 + l])
-            s = s * vm[:, l]
-            z = (s + phi * y) * um[u, l]
-            phis[l, u] = phi
-            sines[l, u] = s
-            if l < 2:
-                k = box(z, m) + BIAS
-        total = jnp.sum(jnp.sum(z, axis=1), axis=1)
-        for v in range(8):
-            partial[v, pl.ds(u, 1), :] = total[v : v + 1]
-        return carry
-
-    lax.fori_loop(0, GROUP, forward, 0, unroll=2)
-
-    tile = jnp.zeros((8, 128), F32)
-    for half in range(2):
-        for j in range(4):
-            for v in range(8):
-                part = partial[v, 8 * half : 8 * half + 8, :]
-                total = jnp.sum(jnp.where(m["group"] == j, part, 0.0), axis=1, keepdims=True)
-                lane = 16 * (2 * (j // 2) + half) + 8 * (j % 2) + v
-                tile = jnp.where(m["lane"] == lane, total, tile)
-    packed[col] = tile * (1.0 / (PIX * PI))
-    packed[col, 0:1, 64 : 64 + CLASSES] = labels_ref[...]
-    loop(1, GROUP, lambda d: tile_col(d, col, col_peer(d)).start())
+    loop(1, GROUP, lambda d: image_row(d, row_peer(d), row).wait_recv())
+    prepare_columns(0)
+
+    def forward(kind):
+        vs = slice(4 * kind, 4 * kind + 4)
+
+        def one(u, carry):
+            k = box(ui[u, 0] * vi[vs, 0] + ui[u, 1] * vi[vs, 1] + ui[u, 2] * vi[vs, 2], m) + BIAS
+            for l in range(3):
+                y = k * um[u, 3 + l]
+                s, phi = arc(y * vm[vs, 3 + l])
+                s = s * vm[vs, l]
+                z = (s + phi * y) * um[u, l]
+                phis[l, u, vs] = phi
+                sines[l, u, vs] = s
+                if l < 2:
+                    k = box(z, m) + BIAS
+            total = jnp.sum(jnp.sum(z, axis=1), axis=1)
+            for v in range(4):
+                partial[4 * kind + v, pl.ds(u, 1), :] = total[v : v + 1]
+            return carry
+
+        lax.fori_loop(0, GROUP, one, 0, unroll=4)
+
+    def pack_tile(kind):
+        tile = jnp.zeros((8, 128), F32)
+        for half in range(2):
+            for j in range(4):
+                for v in range(4):
+                    part = partial[4 * kind + v, 8 * half : 8 * half + 8, :]
+                    total = jnp.sum(jnp.where(m["group"] == j, part, 0.0), axis=1, keepdims=True)
+                    tile = jnp.where(m["lane"] == 16 * half + 4 * j + v, total, tile)
+        return tile * (1.0 / (PIX * PI))
+
+    def assemble(tiles, block):
+        for half in range(2):
+            for h in range(2):
+                acc = jnp.zeros((8, 128), F32)
+                for c in range(8):
+                    moved = tiles[8 * h + c]
+                    turn = (c - half) % 8
+                    if turn:
+                        moved = pltpu.roll(moved, 16 * turn, 1)
+                    acc = jnp.where(m["lane"] // 16 == c, moved, acc)
+                block[h, 8 * half : 8 * half + 8, :] = acc
 
     def backward(u, carry):
         g = box(phis[2, u], m)
@@ -359,34 +380,38 @@
         phis[0, u] = box(g * phis[0, u], m)
         return carry
 
-    lax.fori_loop(0, 6, backward, 0, unroll=2)
+    forward(0)
+    packed[col] = pack_tile(0)
+    packed[col, 0:1, 64 : 64 + CLASSES] = labels_ref[...]
+    far_first(lambda d: tile_col(d, col, col_peer(d)).start())
+    loop(1, GROUP, lambda d: image_tgt(d, row_peer(d), row).wait_recv())
+    prepare_columns(1)
+    forward(1)
+    packed_b[col] = pack_tile(1)
+    far_first(lambda d: tile_col_b(d, col, col_peer(d)).start())
     loop(1, GROUP, lambda d: tile_col(d, col_peer(d), col).wait_recv())
-    slot_of = m["lane"] // 16
-    for kind, block in ((0, send_a), (1, send_b)):
-        for half in range(2):
-            for h in range(2):
-                acc = jnp.zeros((8, 128), F32)
-                for c in range(8):
-                    moved = packed[8 * h + c]
-                    turn = (c - 2 * kind - half) % 8
-                    if turn:
-                        moved = pltpu.roll(moved, 16 * turn, 1)
-                    acc = jnp.where(slot_of == c, moved, acc)
-                block[h, 8 * half : 8 * half + 8, :] = acc
+    assemble(packed, send_a)
+    far_first(lambda d: block_a(d, row, row_peer(d)).start())
+    abuf[:, pl.ds(row * GROUP, GROUP)] = send_a[...]
     for c in range(GROUP):
         send_b[2, c : c + 1, :] = jnp.where(
             m["lane"][0:1] < CLASSES, pltpu.roll(packed[c, 0:1, :], 64, 1), 0.0
         )
-    loop(1, GROUP, lambda d: block_a(d, row, row_peer(d)).start())
-    loop(1, GROUP, lambda d: block_b(d, row, row_peer(d)).start())
-    abuf[:, pl.ds(row * GROUP, GROUP)] = send_a[...]
+    lax.fori_loop(0, BEFORE, backward, 0, unroll=2)
+    loop(1, GROUP, lambda d: tile_col_b(d, col_peer(d), col).wait_recv())
+    assemble(packed_b, send_b)
+    far_first(lambda d: block_b(d, row, row_peer(d)).start())
     bbuf[:, pl.ds(row * GROUP, GROUP)] = send_b[...]
-    lax.fori_loop(6, GROUP, backward, 0, unroll=2)
 
     rows = lax.broadcasted_iota(jnp.int32, (256, 256), 0)
     cols = lax.broadcasted_iota(jnp.int32, (256, 256), 1)
     identity = (rows == cols).astype(F32)
-    permute = (rows == lax.rem(cols, GROUP) * GROUP + cols // GROUP).astype(BF16)
+    there_col = lax.rem(rows, GROUP)
+    there_row = rows // GROUP
+    place = (lax.rem(there_col, 4) * 4 + lax.rem(there_row, 4)) * GROUP + (
+        (there_col // 4) * 4 + there_row // 4
+    )
+    permute = (cols == place).astype(BF16)
     class_row = lax.broadcasted_iota(jnp.int32, (16, 256), 0)
     onehot = (classes_ref[...] == class_row).astype(BF16)
     wanted = jnp.dot(onehot, permute, preferred_element_type=F32) - jnp.where(
@@ -402,7 +427,12 @@
     )
     scale = 1.0 / trace
     system = kss * scale + RIDGE * identity
-    inverse = invert(system, identity)
+
+    def beside(i):
+        if BEFORE + i < GROUP:
+            backward(BEFORE + i, 0)
+
+    inverse = invert(system, identity, beside)
 
     def solve(rhs_t):
         first = dot6(rhs_t, inverse)
@@ -423,18 +453,18 @@
     side2[...] = jnp.transpose(jnp.concatenate([-gamma_t, -alpha_t, alpha_t, pad], axis=0))
     column = side1[pl.ds(col * GROUP, GROUP), :]
     lane16 = lax.broadcasted_iota(jnp.int32, (16, 128), 1)
-    sub16 = lax.broadcasted_iota(jnp.int32, (16, 128), 0)
-    left = jnp.concatenate(
-        [jnp.where(lane16 < 32, column, 0.0), jnp.where(lane16 < 32, 0.0, column)], axis=0
-    )
+    for kind in range(2):
+        masked = jnp.where((lane16 < 32) == (kind == 0), column, 0.0)
+        for j in range(4):
+            wleft[8 * j + 4 * kind : 8 * j + 4 * kind + 4, :] = masked[4 * j : 4 * j + 4]
     right = jnp.concatenate(
         [side2[pl.ds(row, GROUP, stride=GROUP), :], jnp.zeros((112, 128), F32)], axis=0
     )
-    weights = dot_nt(left, right)
-    on_diagonal = ((sub16 == row) & (lane16 == col)).astype(F32)
-    weights = jnp.concatenate(
-        [weights[0:16] - (2.0 * RIDGE / SUPPORT) * inner * on_diagonal, weights[16:32]], axis=0
-    )
+    weights = dot_nt(wleft[...], right)
+    lane32 = lax.broadcasted_iota(jnp.int32, (32, 128), 1)
+    sub32 = lax.broadcasted_iota(jnp.int32, (32, 128), 0)
+    on_diagonal = ((sub32 == 8 * (row // 4) + lax.rem(row, 4)) & (lane32 == col)).astype(F32)
+    weights = weights - (2.0 * RIDGE / SUPPORT) * inner * on_diagonal
     own_row = side1[pl.ds(col * GROUP + row, 1), :]
     label_out[...] = own_row[:, 16 : 16 + CLASSES]
     for u in range(GROUP):
@@ -458,7 +488,8 @@
         return h, jnp.stack(sums[3:], axis=0) * scale_image, ui[u]
 
     def batch(b, last):
-        us = [col_peer(1 + 4 * b + i) for i in range(4)]
+        places = [8 + 2 * b + i // 2 if i % 2 == 0 else 8 - 2 * b - (i + 1) // 2 for i in range(4)]
+        us = [col_peer(d) for d in places]
         parts = [contract(u) for u in us]
         h1, h2, h3 = (jnp.stack([p[0][l] for p in parts], axis=0) for l in range(3))
         back = h1 + box(h2 + box(h3, m) * (1.0 / 9.0), m) * (1.0 / 9.0)
@@ -471,7 +502,7 @@
                 grecv[col] = out[i]
             else:
                 gsend[u] = out[i]
-                grad_col(1 + 4 * b + i, col, u).start()
+                grad_col(places[i], col, u).start()
 
     loop(0, 3, lambda b: batch(b, False))
     batch(3, True)
@@ -479,12 +510,14 @@
     def sent_row(d):
         block_a(d, row, row_peer(d)).wait_send()
         block_b(d, row, row_peer(d)).wait_send()
-        image_col(mine, d, col, col_peer(d)).wait_send()
+        image_col(d, col, col_peer(d)).wait_send()
+        image_row(d, row, row_peer(d)).wait_send()
+        image_tgt(d, row, row_peer(d)).wait_send()
         tile_col(d, col, col_peer(d)).wait_send()
+        tile_col_b(d, col, col_peer(d)).wait_send()
         grad_col(d, col, col_peer(d)).wait_send()
 
     loop(1, GROUP, sent_row)
-    loop(0, GROUP - 1, lambda k: image_row(own, k, row, sibling).wait_send())
     loop(1, GROUP, lambda d: grad_col(d, col_peer(d), col).wait_recv())
     total = grecv[0]
     for i in range(1, GROUP):
@@ -520,17 +553,19 @@
             buf(3, GROUP, 8, 4, 8, 128),
             buf(8, GROUP, 128),
             buf(GROUP, 8, 128),
+            buf(GROUP, 8, 128),
             buf(2, GROUP, 128),
             buf(3, GROUP, 128),
             buf(2, 256, 128),
             buf(3, 256, 128),
             buf(256, 128),
             buf(256, 128),
+            buf(32, 128),
             buf(GROUP, 8, 128),
             buf(GROUP, 3, 8, 128),
             buf(GROUP, 3, 8, 128),
         ]
-        + [pltpu.SemaphoreType.DMA((GROUP,))] * 12,
+        + [pltpu.SemaphoreType.DMA((GROUP,))] * 16,
         compiler_params=pltpu.CompilerParams(
             collective_id=0, has_side_effects=True, vmem_limit_bytes=56 << 20
         ),

time: 72.4 us -> 64.4 us (0.89)
  Pallas kernels: 66.6 us -> 58.7 us
    pallas_call x1, Pallas kernels: 66.6 us -> 58.7 us  [body(): pl.pallas_call(step_kernel, name='kip_step', out_shape=(jax.ShapeDtypeStr...]
where the time goes in v3:
time: 64.4 us; the launch traced here: 64.2 us
  Pallas kernels  58.7 us (91%)
  between operations  3.68 us (6%)
  local copies, waits for them, and re-layouts  1.82 us (3%)
    pallas_call x1, Pallas kernels, body(): pl.pallas_call(step_kernel, name='kip_step', out_shape=(jax.ShapeDtypeStr...  58.7 us
    unnamed x4, local copies, waits for them, and re-layouts  1.82 us

profile of v3, /device:TPU:1, one launch (start us, length us, event | category | flops | bytes accessed | tf_op | source)
XLA Modules:
  0.0 64.2 jit_solution(6920819582178056679)
XLA Ops:
  1.9 58.7 %kip_step.1 = (f32[3,1,1024]{2,1,0:T(1,128)}, f32[1,10]{1,0:T(1,128)}, f32[1,1]{1,0:T(1,128)}) custom-call(f32[1,3,4,1024]{3,2,1,0:T(4,128)} %bitcast.5, s32[1]{0:T(128)S(6)} %copy.12.pick_ref, f32[1,3,4,1024]{3,2,1,0:T(4,128)} %bitcast.6, s32[1]{0:T(128)S(6)} %copy.13.target_pick_ref, f32[1,10]{1,0:T(1,128)} %labels_ref.1, s32[1,256]{1,0:T(1,128)} %bitcast.8), custom_call_target="tpu_custom_call" | custom-call | tf_op jit(solution)/shard_map/kip_step/pallas_call | solution.py:534
  60.6 0.0 copy-start
  60.6 1.3 %copy.14 = f32[1,3,1024]{2,0,1:T(1,128)} copy(f32[1,3,1024]{2,0,1:T(1,128)} %bitcast.7) | data formatting | bytes 24576
  62.0 0.0 copy-done
  62.0 0.5 copy.15
Async XLA Ops:
  60.6 1.3 %copy-start = (f32[1,10]{1,0:T(1,128)S(1)}, f32[1,10]{1,0:T(1,128)}, u32[]{:S(2)}) copy-start(f32[1,10]{1,0:T(1,128)} %get-tuple-element.13) | copy-start | bytes 124

commit v4 on v3

--- a/solution.py
+++ b/solution.py
@@ -40,6 +40,7 @@
 
 FIRST_SCALE, SCALES = inverse_schedule()
 BEFORE = 10
+SPLIT = 8
 assert GROUP - BEFORE <= 2 * (len(SCALES) - 1)
 
 
@@ -148,7 +149,7 @@
     x = (SCALES[0] * FIRST_SCALE) * (2.0 * identity - FIRST_SCALE * a)
     count = len(SCALES)
     for i in range(1, count):
-        mul = dot6 if i == count - 1 else dot3
+        mul = dot6 if i >= count - 1 else dot3
         product = mul(a, x)
         beside(2 * i - 2)
         x = SCALES[i] * mul(x, 2.0 * identity - product)
@@ -329,7 +330,7 @@
     loop(1, GROUP, lambda d: image_row(d, row_peer(d), row).wait_recv())
     prepare_columns(0)
 
-    def forward(kind):
+    def forward(kind, low, high):
         vs = slice(4 * kind, 4 * kind + 4)
 
         def one(u, carry):
@@ -348,7 +349,7 @@
                 partial[4 * kind + v, pl.ds(u, 1), :] = total[v : v + 1]
             return carry
 
-        lax.fori_loop(0, GROUP, one, 0, unroll=4)
+        lax.fori_loop(low, high, one, 0, unroll=4)
 
     def pack_tile(kind):
         tile = jnp.zeros((8, 128), F32)
@@ -380,23 +381,24 @@
         phis[0, u] = box(g * phis[0, u], m)
         return carry
 
-    forward(0)
+    forward(0, 0, GROUP)
     packed[col] = pack_tile(0)
     packed[col, 0:1, 64 : 64 + CLASSES] = labels_ref[...]
     far_first(lambda d: tile_col(d, col, col_peer(d)).start())
     loop(1, GROUP, lambda d: image_tgt(d, row_peer(d), row).wait_recv())
     prepare_columns(1)
-    forward(1)
+    forward(1, 0, SPLIT)
+    loop(1, GROUP, lambda d: tile_col(d, col_peer(d), col).wait_recv())
+    assemble(packed, send_a)
+    for c in range(GROUP):
+        send_a[2, c : c + 1, :] = jnp.where(
+            m["lane"][0:1] < CLASSES, pltpu.roll(packed[c, 0:1, :], 64, 1), 0.0
+        )
+    far_first(lambda d: block_a(d, row, row_peer(d)).start())
+    abuf[:, pl.ds(row * GROUP, GROUP)] = send_a[...]
+    forward(1, SPLIT, GROUP)
     packed_b[col] = pack_tile(1)
     far_first(lambda d: tile_col_b(d, col, col_peer(d)).start())
-    loop(1, GROUP, lambda d: tile_col(d, col_peer(d), col).wait_recv())
-    assemble(packed, send_a)
-    far_first(lambda d: block_a(d, row, row_peer(d)).start())
-    abuf[:, pl.ds(row * GROUP, GROUP)] = send_a[...]
-    for c in range(GROUP):
-        send_b[2, c : c + 1, :] = jnp.where(
-            m["lane"][0:1] < CLASSES, pltpu.roll(packed[c, 0:1, :], 64, 1), 0.0
-        )
     lax.fori_loop(0, BEFORE, backward, 0, unroll=2)
     loop(1, GROUP, lambda d: tile_col_b(d, col_peer(d), col).wait_recv())
     assemble(packed_b, send_b)
@@ -434,18 +436,17 @@
 
     inverse = invert(system, identity, beside)
 
-    def solve(rhs_t):
-        first = dot6(rhs_t, inverse)
-        return (first + dot6(rhs_t - dot6(first, system), inverse)) * scale
-
+    labels_t = jnp.transpose(ordered(abuf, 2))[0:16]
+    alpha_t = dot6(labels_t, inverse)
+    alpha_t = (alpha_t + dot6(labels_t - dot6(alpha_t, system), inverse)) * scale
     loop(1, GROUP, lambda d: block_b(d, row_peer(d), row).wait_recv())
-    labels_t = jnp.transpose(ordered(bbuf, 2))[0:16]
     kst = jnp.concatenate([ordered(bbuf, 0), ordered(bbuf, 1)], axis=1)
-    alpha_t = solve(labels_t)
     error_t = dot6(alpha_t, kst) - wanted
     loss = jnp.sum(jnp.sum(error_t * error_t, axis=0, keepdims=True), axis=1, keepdims=True)
     loss_out[...] = 0.5 * loss
-    gamma_t = solve(dot_nt(error_t, kst))
+    rhs_t = dot_nt(error_t, kst)
+    gamma_t = dot6(rhs_t, inverse)
+    gamma_t = (gamma_t + dot6(rhs_t - dot6(gamma_t, system), inverse)) * scale
     inner = jnp.sum(jnp.sum(gamma_t * alpha_t, axis=0, keepdims=True), axis=1, keepdims=True)
 
     pad = jnp.zeros((80, 256), F32)
@@ -554,10 +555,10 @@
             buf(8, GROUP, 128),
             buf(GROUP, 8, 128),
             buf(GROUP, 8, 128),
+            buf(3, GROUP, 128),
             buf(2, GROUP, 128),
-            buf(3, GROUP, 128),
+            buf(3, 256, 128),
             buf(2, 256, 128),
-            buf(3, 256, 128),
             buf(256, 128),
             buf(256, 128),
             buf(32, 128),

time: 64.4 us -> 63.7 us (0.989)
  Pallas kernels: 58.7 us -> 58 us
    pallas_call x1, Pallas kernels: 58.7 us -> 58 us  [body(): pl.pallas_call(step_kernel, name='kip_step', out_shape=(jax.ShapeDtypeStr...]
where the time goes in v4:
time: 63.7 us; the launch traced here: 63.5 us
  Pallas kernels  58 us (91%)
  between operations  3.68 us (6%)
  local copies, waits for them, and re-layouts  1.82 us (3%)
    pallas_call x1, Pallas kernels, body(): pl.pallas_call(step_kernel, name='kip_step', out_shape=(jax.ShapeDtypeStr...  58 us
    unnamed x4, local copies, waits for them, and re-layouts  1.82 us

profile of v4, /device:TPU:1, one launch (start us, length us, event | category | flops | bytes accessed | tf_op | source)
XLA Modules:
  0.0 63.5 jit_solution(5841010701753601932)
XLA Ops:
  1.9 58.0 %kip_step.1 = (f32[3,1,1024]{2,1,0:T(1,128)}, f32[1,10]{1,0:T(1,128)}, f32[1,1]{1,0:T(1,128)}) custom-call(f32[1,3,4,1024]{3,2,1,0:T(4,128)} %bitcast.5, s32[1]{0:T(128)S(6)} %copy.12.pick_ref, f32[1,3,4,1024]{3,2,1,0:T(4,128)} %bitcast.6, s32[1]{0:T(128)S(6)} %copy.13.target_pick_ref, f32[1,10]{1,0:T(1,128)} %labels_ref.1, s32[1,256]{1,0:T(1,128)} %bitcast.8), custom_call_target="tpu_custom_call" | custom-call | tf_op jit(solution)/shard_map/kip_step/pallas_call | solution.py:535
  59.9 0.0 copy-start
  59.9 1.3 %copy.14 = f32[1,3,1024]{2,0,1:T(1,128)} copy(f32[1,3,1024]{2,0,1:T(1,128)} %bitcast.7) | data formatting | bytes 24576
  61.3 0.0 copy-done
  61.3 0.5 copy.15
Async XLA Ops:
  59.9 1.3 %copy-start = (f32[1,10]{1,0:T(1,128)S(1)}, f32[1,10]{1,0:T(1,128)}, u32[]{:S(2)}) copy-start(f32[1,10]{1,0:T(1,128)} %get-tuple-element.13) | copy-start | bytes 124

commit v5 on v4

--- a/solution.py
+++ b/solution.py
@@ -305,7 +305,6 @@
     far_first(lambda d: image_tgt(d, row, row_peer(d)).start())
     vraw[row] = own[...]
     uraw[col] = own[0:3]
-    loop(1, GROUP, lambda d: image_col(d, col_peer(d), col).wait_recv())
 
     def prepare_rows(i):
         us = pl.ds(i * 4, 4)
@@ -316,7 +315,22 @@
             um[us, l] = d * r * (1.0 / (9.0 * PI) if l < 2 else 1.0)
             um[us, 3 + l] = r
 
-    loop(0, 4, prepare_rows)
+    def landed_rows(i):
+        group = lax.rem(col // 4 + i, 4)
+
+        def landed(k):
+            slot = 4 * group + k
+
+            @pl.when(slot != col)
+            def _():
+                image_col(0, slot, col).wait_recv()
+
+        loop(0, 4, landed)
+        prepare_rows(group)
+
+    for i in (0, 1, 3, 2):
+        landed_rows(i)
+
 
     def prepare_columns(kind):
         vs = slice(4 * kind, 4 * kind + 4)
@@ -439,6 +453,16 @@
     labels_t = jnp.transpose(ordered(abuf, 2))[0:16]
     alpha_t = dot6(labels_t, inverse)
     alpha_t = (alpha_t + dot6(labels_t - dot6(alpha_t, system), inverse)) * scale
+
+    def sent_early(d):
+        image_col(d, col, col_peer(d)).wait_send()
+        image_row(d, row, row_peer(d)).wait_send()
+        image_tgt(d, row, row_peer(d)).wait_send()
+        tile_col(d, col, col_peer(d)).wait_send()
+        tile_col_b(d, col, col_peer(d)).wait_send()
+        block_a(d, row, row_peer(d)).wait_send()
+
+    loop(1, GROUP, sent_early)
     loop(1, GROUP, lambda d: block_b(d, row_peer(d), row).wait_recv())
     kst = jnp.concatenate([ordered(bbuf, 0), ordered(bbuf, 1)], axis=1)
     error_t = dot6(alpha_t, kst) - wanted
@@ -508,17 +532,11 @@
     loop(0, 3, lambda b: batch(b, False))
     batch(3, True)
 
-    def sent_row(d):
-        block_a(d, row, row_peer(d)).wait_send()
+    def sent_late(d):
         block_b(d, row, row_peer(d)).wait_send()
-        image_col(d, col, col_peer(d)).wait_send()
-        image_row(d, row, row_peer(d)).wait_send()
-        image_tgt(d, row, row_peer(d)).wait_send()
-        tile_col(d, col, col_peer(d)).wait_send()
-        tile_col_b(d, col, col_peer(d)).wait_send()
         grad_col(d, col, col_peer(d)).wait_send()
 
-    loop(1, GROUP, sent_row)
+    loop(1, GROUP, sent_late)
     loop(1, GROUP, lambda d: grad_col(d, col_peer(d), col).wait_recv())
     total = grecv[0]
     for i in range(1, GROUP):

time: 63.7 us -> 63.7 us (level)
  no operation moved by 1% of the time
where the time goes in v5:
time: 63.7 us; the launch traced here: 63.4 us
  Pallas kernels  58 us (91%)
  between operations  3.68 us (6%)
  local copies, waits for them, and re-layouts  1.82 us (3%)
    pallas_call x1, Pallas kernels, body(): pl.pallas_call(step_kernel, name='kip_step', out_shape=(jax.ShapeDtypeStr...  58 us
    unnamed x4, local copies, waits for them, and re-layouts  1.82 us

profile of v5, /device:TPU:1, one launch (start us, length us, event | category | flops | bytes accessed | tf_op | source)
XLA Modules:
  0.0 63.4 jit_solution(1350669242721646446)
XLA Ops:
  1.9 58.0 %kip_step.1 = (f32[3,1,1024]{2,1,0:T(1,128)}, f32[1,10]{1,0:T(1,128)}, f32[1,1]{1,0:T(1,128)}) custom-call(f32[1,3,4,1024]{3,2,1,0:T(4,128)} %bitcast.5, s32[1]{0:T(128)S(6)} %copy.12.pick_ref, f32[1,3,4,1024]{3,2,1,0:T(4,128)} %bitcast.6, s32[1]{0:T(128)S(6)} %copy.13.target_pick_ref, f32[1,10]{1,0:T(1,128)} %labels_ref.1, s32[1,256]{1,0:T(1,128)} %bitcast.8), custom_call_target="tpu_custom_call" | custom-call | tf_op jit(solution)/shard_map/kip_step/pallas_call | solution.py:553
  59.9 0.0 copy-start
  59.9 1.3 %copy.14 = f32[1,3,1024]{2,0,1:T(1,128)} copy(f32[1,3,1024]{2,0,1:T(1,128)} %bitcast.7) | data formatting | bytes 24576
  61.2 0.0 copy-done
  61.2 0.5 copy.15
Async XLA Ops:
  59.9 1.3 %copy-start = (f32[1,10]{1,0:T(1,128)S(1)}, f32[1,10]{1,0:T(1,128)}, u32[]{:S(2)}) copy-start(f32[1,10]{1,0:T(1,128)} %get-tuple-element.13) | copy-start | bytes 124
